TPU v7x, 512 devices: a whole 4x8x8 slice. The times are simulated.
512 devices in a mesh: patch: 128 (over z, y, core), det: 4 (over x).
Axes of the slice: x: 4, y: 8, z: 8, core: 2. Of those that a mesh axis runs over, the one named last changes fastest.
Arguments:
- strips: bfloat16 [12288, 4, 2048], P('patch', None, 'det'), may hold values from -16 to 16
- strip_patch: int32 [12288], P('patch'), may hold values from 0 to 127, as said below
- strip_row: int32 [12288], P('patch'), may hold values from 0 to 24
- strip_weight: bfloat16 [12288], P('patch'), may hold values from 0.25 to 4
- science: float32 [128, 8, 2048], P('patch', None, 'det'), may hold values from -32 to 32
Outputs:
- difference: float32 [128, 8, 2048], P('patch', None, 'det')
- coefficients: float32 [128, 4, 46], P('patch', 'det')
Inputs may be any that keep to these rules, and one draw needn't show every extreme that they name: `strip_patch`: among the 96 strips of one index of patch (aligned blocks), no patch is named more than 2 times; one patch, the same for every block, is named exactly 2 times in every block.
All inputs are finite; a program needn't handle non-finite values.
Results may differ from a plain program's by a relative error of at most 0.00055.
Values may be sent and summed in bfloat16 or wider, within the bound.
No kernel may reach another device: no remote copies, remote signals or barrier semaphores. Data moves between devices by JAX's collectives and lax.ppermute only.
A program may use at most 64 MiB of HBM per device.

v0:
```python
import jax
import jax.numpy as jnp
from jax import lax
from jax.sharding import PartitionSpec as P

BASIS = 45


SIGMAS = (0.7, 1.5, 3.0)
RIDGE = 0.01


def padded_2(x, sides, width):
    for axis, dim in sides:
        devices, length = (lax.axis_size(axis), x.shape[dim])
        up = [(i, (i + 1) % devices) for i in range(devices - 1)]
        down = [(j, i) for i, j in up]
        last = lax.slice_in_dim(x, length - width, length, axis=dim)
        first = lax.slice_in_dim(x, 0, width, axis=dim)
        before = lax.ppermute(last, axis, up)
        after = lax.ppermute(first, axis, down)
        x = jnp.concatenate([before, x, after], axis=dim)
    return x


def basis_tables():
    tap_offsets = jnp.arange(21, dtype=jnp.float32) - 10.0
    profiles = []
    for gauss_width in SIGMAS:
        for degree in range(5):
            scaled = tap_offsets / gauss_width
            profile = scaled**degree * jnp.exp(-0.5 * scaled * scaled)
            profiles.append(profile / jnp.sqrt(jnp.sum(profile * profile)))
    kernels = jnp.stack(profiles)
    col_pick = []
    row_pick = []
    for s in range(3):
        for i in range(5):
            for j in range(5 - i):
                col_pick.append(5 * s + i)
                row_pick.append(5 * s + j)
    return (kernels, col_pick, row_pick)


def row_matrices(kernels, row_pick, out_rows, in_rows):
    reach = (
        jnp.arange(in_rows, dtype=jnp.int32)[None, :]
        - jnp.arange(out_rows, dtype=jnp.int32)[:, None]
    )
    onehot = (reach[:, :, None] == jnp.arange(21, dtype=jnp.int32)[None, None, :]).astype(
        jnp.float32
    )
    chosen = jnp.stack([kernels[r] for r in row_pick])
    return jnp.einsum("ka,ota->kot", chosen, onehot, precision=lax.Precision.HIGHEST)


def solve_normal(normal, target):
    unknowns = normal.shape[0]
    ridge_shift = RIDGE * jnp.trace(normal) / unknowns
    system = normal + ridge_shift * jnp.eye(unknowns, dtype=normal.dtype)
    factor = jnp.linalg.cholesky(system)
    forward = lax.linalg.triangular_solve(factor, target[:, None], left_side=True, lower=True)
    backward = lax.linalg.triangular_solve(
        factor, forward, left_side=True, lower=True, transpose_a=True
    )
    return backward[:, 0]


def body(strips, strip_patch, strip_row, strip_weight, science):
    peer_count = lax.axis_size("patch")
    strip_count, strip_rows, columns = strips.shape
    out_rows = science.shape[1]
    template_rows = out_rows + 20
    landing = (strip_patch * template_rows + strip_row)[:, None] + jnp.arange(
        strip_rows, dtype=jnp.int32
    )[None, :]
    weighted = strips.astype(jnp.float32) * strip_weight.astype(jnp.float32)[:, None, None]
    partial_value = jnp.zeros((peer_count * template_rows, columns), jnp.float32)
    partial_value = partial_value.at[landing.reshape(-1)].add(weighted.reshape(-1, columns))
    partial_cover = jnp.zeros((peer_count * template_rows,), jnp.float32)
    partial_cover = partial_cover.at[landing.reshape(-1)].add(
        jnp.repeat(strip_weight.astype(jnp.float32), strip_rows)
    )
    received, received_cover = (
        lax.all_to_all(
            partial_value.reshape(peer_count, template_rows, columns),
            "patch",
            split_axis=0,
            concat_axis=0,
            tiled=True,
        ),
        lax.all_to_all(
            partial_cover.reshape(peer_count, template_rows),
            "patch",
            split_axis=0,
            concat_axis=0,
            tiled=True,
        ),
    )
    numerator = jnp.sum(received, axis=0)
    coverage = jnp.sum(received_cover, axis=0)
    template = numerator / (1.0 + coverage)[:, None]
    padded = padded_2(template, (("det", 1),), 10)
    kernels, col_pick, row_pick = basis_tables()
    rowmats = row_matrices(kernels, row_pick, out_rows, template_rows)
    shifted = jnp.stack([padded[:, a : a + columns] for a in range(21)])
    colconv = jnp.einsum("ka,atw->ktw", kernels, shifted, precision=lax.Precision.HIGHEST)
    picked = jnp.stack([colconv[c] for c in col_pick])
    basis_images = jnp.einsum("kot,ktw->kow", rowmats, picked, precision=lax.Precision.HIGHEST)
    pixels = out_rows * columns
    design = jnp.concatenate(
        [basis_images.reshape(BASIS, pixels), jnp.ones((1, pixels), jnp.float32)], axis=0
    )
    normal = jnp.dot(design, design.T, precision=lax.Precision.HIGHEST)
    target = jnp.dot(design, science.reshape(pixels), precision=lax.Precision.HIGHEST)
    fitted = solve_normal(normal, target)
    model_image = jnp.dot(fitted, design, precision=lax.Precision.HIGHEST).reshape(
        1, out_rows, columns
    )
    return (science - model_image, fitted[None, None, :])


def solution(mesh):
    placed = (P("patch", None, "det"), P("patch"), P("patch"), P("patch"), P("patch", None, "det"))
    return jax.shard_map(
        body,
        mesh=mesh,
        in_specs=placed,
        out_specs=(P("patch", None, "det"), P("patch", "det", None)),
        check_vma=False,
    )
```

profile of v0, /device:TPU:154, one launch (start us, length us, event | category | flops | bytes accessed | tf_op | source)
XLA Modules:
  0.0 354.9 jit_solution(17642329803127371207)
XLA Ops:
  1.5 0.7 broadcast_in_dim.12
  2.4 3.6 %scatter_custom_fusion.1 = f32[3584]{0:T(1024)S(1)} fusion(s32[384]{0:T(512)S(1)} %fusion.56, f32[384]{0:T(512)S(1)} %reshape.306, f32[]{:T(128)} %constant.73.clone.1), kind=kCustom, calls=%fused_computation.111 | custom fusion | flops 384 | bytes 14340 | tf_op jit(solution)/shard_map/scatter-add | solution.py:81
  6.7 15.5 %all-to-all-start.1 = ((f32[128,1,28]{2,1,0:T(1,128)}), f32[128,1,28]{2,1,0:T(1,128)S(1)}, u32[]{:S(2)}, u32[]{:S(2)}) async-start(f32[128,1,28]{2,1,0:T(1,128)} %bitcast.2), calls=%async_computation.1 | async-start | bytes 131072 | tf_op jit(solution)/shard_map/all_to_all | solution.py:92
  22.9 1.2 convert_multiply_fusion
  24.3 6.3 %scatter_custom_fusion = f32[3584,512]{1,0:T(8,128)} fusion(s32[384]{0:T(512)S(1)} %fusion.56, f32[384,512]{1,0:T(8,128)S(1)} %reshape.298, f32[]{:T(128)} %constant.73.clone.1), kind=kCustom, calls=%fused_computation.2 | custom fusion | flops 196608 | bytes 7340036 | tf_op jit(solution)/shard_map/scatter-add | solution.py:79
  30.6 8.9 %reshape.289 = f32[128,28,512]{2,1,0:T(8,128)} reshape(f32[3584,512]{1,0:T(8,128)} %scatter_custom_fusion) | data formatting | bytes 14680064 | tf_op jit(solution)/shard_map/reshape | solution.py:86
  39.5 14.3 %all-to-all-start = ((f32[128,28,512]{2,1,0:T(8,128)}), f32[128,28,512]{2,1,0:T(8,128)}, u32[]{:S(2)}, u32[]{:S(2)}) async-start(f32[128,28,512]{2,1,0:T(8,128)} %reshape.289), calls=%async_computation | async-start | bytes 16777216 | tf_op jit(solution)/shard_map/all_to_all | solution.py:85
  74.2 0.8 copy.98
  75.8 228.3 %all-to-all-done = f32[128,28,512]{2,1,0:T(8,128)} async-done(((f32[128,28,512]{2,1,0:T(8,128)}), f32[128,28,512]{2,1,0:T(8,128)}, u32[]{:S(2)}, u32[]{:S(2)}) %all-to-all-start) | async-done | bytes 7340064 | tf_op jit(solution)/shard_map/all_to_all | solution.py:85
  304.2 4.1 %reduce_sum.180 = f32[28,512]{1,0:T(8,128)S(1)} reduce(f32[128,28,512]{2,1,0:T(8,128)} %all-to-all-done, f32[]{:T(128)} %constant.73.clone.1), dimensions={0}, to_apply=%region_16.0 | reduce | flops 1820672 | bytes 7397380 | tf_op jit(solution)/shard_map/reduce_sum | solution.py:100
  308.4 3.4 collective-permute-start
  311.8 2.6 collective-permute-start.1
  314.6 2.8 collective-permute-done.1
  319.4 2.0 stack.111
  321.4 0.9 fusion.52
  322.3 1.3 fusion.67
  323.5 1.0 fusion.68
  324.7 11.5 %stack.112 = f32[45,28,512]{2,0,1:T(8,128)S(1)} concatenate(f32[1,28,512]{2,0,1:T(1,128)S(1)} %get-tuple-element.20, f32[1,28,512]{2,0,1:T(1,128)S(1)} %get-tuple-element.20, f32[1,28,512]{2,0,1:T(1,128)S(1)} %get-tuple-element.20, f32[1,28,512]{2,0,1:T(1,128)S(1)} %get-tuple-element.20, f32[2,28,512]{2,0,1:T(2,128)} %get-tuple-element.11, f32[1,28,512]{2,0,1:T(1,128)S(1)} %get-tuple-element.19, ...), dimensions={0} | concatenate | bytes 5160960 | tf_op jit(solution)/shard_map/stack | solution.py:108
  336.1 3.9 %fusion.2 = f32[45,8,512]{2,1,0:T(8,128)S(1)} fusion(f32[45,8,28]{2,1,0:T(8,128)} %copy.98, f32[45,28,512]{2,0,1:T(8,128)S(1)} %stack.112), kind=kOutput, calls=%fused_computation.4 | convolution fusion | flops 61931520 | bytes 3358080 | tf_op jit(solution)/shard_map/kot,ktw->kow/dot_general | solution.py:109
  340.5 1.4 select_reduce_fusion.1
  342.7 4.2 %cholesky.17 = f32[46,46]{1,0:T(8,128)S(1)} custom-call(f32[46,46]{1,0:T(8,128)S(1)} %fusion.50), custom_call_target="Cholesky" | custom-call | tf_op jit(solution)/shard_map/jit(cholesky)/cholesky | solution.py:61
  348.2 3.5 custom-call.8
  351.7 0.7 convolution_bitcast_fusion.1
  353.4 0.9 fusion.4
  (89 shorter events, 19.0 us)
Async XLA Ops:
  6.7 32.8 %all-to-all-start.1 = ((f32[128,1,28]{2,1,0:T(1,128)}), f32[128,1,28]{2,1,0:T(1,128)S(1)}, u32[]{:S(2)}, u32[]{:S(2)}) async-start(f32[128,1,28]{2,1,0:T(1,128)} %bitcast.2), calls=%async_computation.1 | async-start | bytes 131072 | tf_op jit(solution)/shard_map/all_to_all | solution.py:92
  39.5 35.5 %copy-start = (f32[1,8,512]{2,1,0:T(8,128)S(1)}, f32[1,8,512]{2,1,0:T(8,128)}, u32[]{:S(2)}) copy-start(f32[1,8,512]{2,1,0:T(8,128)} %param.9) | copy-start | bytes 49156
  39.5 264.6 %all-to-all-start = ((f32[128,28,512]{2,1,0:T(8,128)}), f32[128,28,512]{2,1,0:T(8,128)}, u32[]{:S(2)}, u32[]{:S(2)}) async-start(f32[128,28,512]{2,1,0:T(8,128)} %reshape.289), calls=%async_computation | async-start | bytes 16777216 | tf_op jit(solution)/shard_map/all_to_all | solution.py:85
  308.4 6.2 %collective-permute-start = (f32[28,10]{1,0:T(8,128)S(1)}, f32[28,10]{1,0:T(8,128)S(1)}, u32[]{:S(2)}, u32[]{:S(2)}) collective-permute-start(f32[28,10]{1,0:T(8,128)S(1)} %get-tuple-element.44), channel_id=1, source_target_pairs={{0,1},{1,2},{2,3},{4,5},{5,6},{6,7},{8,9},{9,10},{10,11},{12,13},{... | collective-permute-start | bytes 3368 | tf_op jit(solution)/shard_map/ppermute | solution.py:20
  311.8 5.6 %collective-permute-start.1 = (f32[28,10]{1,0:T(8,128)S(1)}, f32[28,10]{1,0:T(8,128)S(1)}, u32[]{:S(2)}, u32[]{:S(2)}) collective-permute-start(f32[28,10]{1,0:T(8,128)S(1)} %get-tuple-element.43), channel_id=1, source_target_pairs={{1,0},{2,1},{3,2},{5,4},{6,5},{7,6},{9,8},{10,9},{11,10},{13,12},{... | collective-permute-start | bytes 3368 | tf_op jit(solution)/shard_map/ppermute | solution.py:21
  340.0 11.7 %copy-start.2 = (f32[1,1,8,512]{3,1,2,0:T(1,128)S(1)}, f32[1,1,8,512]{3,1,2,0:T(1,128)}, u32[]{:S(2)}) copy-start(f32[1,1,8,512]{3,1,2,0:T(1,128)} %copy.106) | copy-start | bytes 49156
  352.5 1.8 copy-start.1
  352.8 2.1 copy-start.3
where the time goes:
time: 356 us; the launch traced here: 355 us
  waiting for transfers between devices  231 us (65%)
  other arithmetic  36.6 us (10%)
  starting transfers between devices  35.8 us (10%)
  local copies, waits for them, and re-layouts  30.9 us (9%)
  between operations  12.1 us (3%)
  matrix products  8.37 us (2%)
    all_to_all x1, waiting for transfers between devices, body(): lax.all_to_all(partial_value.reshape(peer_count, template_rows, columns),...  228 us
    all_to_all x1, starting transfers between devices, body(): lax.all_to_all(partial_cover.reshape(peer_count, template_rows), 'patch',...  15.5 us
    all_to_all x1, starting transfers between devices, body(): lax.all_to_all(partial_value.reshape(peer_count, template_rows, columns),...  14.3 us
    another operation x1, local copies, waits for them, and re-layouts, body(): picked = jnp.stack([colconv[c] for c in col_pick])  11.5 us
    reduce_sum x15, other arithmetic, basis_tables(): profiles.append(profile / jnp.sqrt(jnp.sum(profile * profile)))  9.29 us
    reshape x1, local copies, waits for them, and re-layouts, body(): partial_value.reshape(peer_count, template_rows, columns)  8.94 us
  transfers between devices with their start and end apart: 4, of which 2 were waited for; matrix products, arithmetic and copies ran while one was open for 8% of the time, Pallas kernels for 0%

commit v1 on v0

v1 whole, which is shorter than its diff:
```python
import jax
import jax.numpy as jnp
import numpy as np
from jax import lax
from jax.experimental import pallas as pl
from jax.experimental.pallas import tpu as pltpu
from jax.sharding import PartitionSpec as P

BASIS = 45
SIGMAS = (0.7, 1.5, 3.0)
RIDGE = 0.01
TAPS = 21
REACH = 10
ROWS = 8
TROWS = 32
SLOTS = 8
EXTRA = 128
ONE = 32
KP = 48
UNKNOWNS = BASIS + 1
F32 = jnp.float32
BF16 = jnp.bfloat16


def tap_table():
    offsets = np.arange(TAPS, dtype=np.float64) - REACH
    profiles = []
    for width in SIGMAS:
        for degree in range(5):
            scaled = offsets / width
            profile = scaled**degree * np.exp(-0.5 * scaled * scaled)
            profiles.append(profile / np.sqrt(np.sum(profile * profile)))
    table = np.zeros((ROWS, KP, TAPS, TROWS))
    k = 0
    for s in range(3):
        for i in range(5):
            for j in range(5 - i):
                kernel = np.outer(profiles[5 * s + i], profiles[5 * s + j])
                for o in range(ROWS):
                    table[o, k, :, o : o + TAPS] = kernel
                k += 1
    table = table.reshape(ROWS * KP, TAPS * TROWS).astype(np.float32)
    high = table.astype(BF16)
    low = (table - high.astype(np.float32)).astype(BF16)
    return high, low


def iota(shape, dim):
    return lax.broadcasted_iota(jnp.int32, shape, dim)


def split(x):
    high = x.astype(BF16)
    return high, (x - high.astype(F32)).astype(BF16)


def pack_kernel(strips_ref, patch_ref, row_ref, weight_ref, out_ref):
    count = patch_ref.shape[1]
    lines = strips_ref.shape[0]
    columns = strips_ref.shape[1]
    reps = lines // count
    first, second = iota((count, count), 0), iota((count, count), 1)
    patch = jnp.broadcast_to(patch_ref[...], (count, count))
    patch_col = jnp.sum(jnp.where(first == second, patch, 0).astype(F32), axis=1, keepdims=True)
    earlier = (patch.astype(F32) == patch_col) & (first < second)
    occurrence = jnp.sum(jnp.where(earlier, 1.0, 0.0), axis=0, keepdims=True)
    place = 2.0 * patch_ref[...].astype(F32) + occurrence
    spread = (iota((count, lines), 1) // reps == iota((count, lines), 0)).astype(F32).astype(BF16)
    wide = jnp.dot(
        jnp.broadcast_to(place, (8, count)).astype(BF16), spread, preferred_element_type=F32
    )[:1]
    key = wide.astype(jnp.int32) * reps + iota((1, lines), 1) % reps
    here = iota((lines, count), 0) // reps == iota((lines, count), 1)
    row = jnp.sum(
        jnp.where(here, row_ref[...].astype(F32), 0.0), axis=1, keepdims=True
    ).astype(jnp.int32)
    weight = jnp.sum(jnp.where(here, weight_ref[...], 0.0), axis=1, keepdims=True)
    lane = iota((lines, EXTRA), 1)
    at = row + iota((lines, EXTRA), 0) % reps
    extra = jnp.where(lane == at, weight, jnp.where(lane == ONE, 1.0, 0.0)).astype(BF16)
    strips = strips_ref[...]
    total = out_ref.shape[0]
    step = 256
    for base in range(0, total, step):
        pick = (iota((step, lines), 0) + base == key).astype(F32).astype(BF16)
        out_ref[base : base + step, :columns] = jnp.dot(
            pick, strips, preferred_element_type=F32
        ).astype(BF16)
        out_ref[base : base + step, columns:] = jnp.dot(
            pick, extra, preferred_element_type=F32
        ).astype(BF16)


def template_kernel(received_ref, template_ref, first_ref, last_ref):
    columns = template_ref.shape[1]
    spread = received_ref[:, columns:]
    sums = lax.dot_general(
        spread, received_ref[...], (((0,), (0,)), ((), ())), preferred_element_type=F32
    )[:TROWS]
    coverage = sums[:, columns + ONE : columns + ONE + 1]
    template = sums[:, :columns] / (1.0 + coverage)
    template_ref[...] = template
    first_ref[...] = template[:, :128]
    last_ref[...] = template[:, columns - 128 :]


def fit_kernel(
    template_ref, before_ref, after_ref, science_ref, high_ref, low_ref,
    difference_ref, coefficients_ref, design_ref, parts_ref,
):
    columns = template_ref.shape[1]
    padded = jnp.concatenate([before_ref[...], template_ref[...], after_ref[...]], axis=1)
    upper, lower = split(padded)
    left = 128 - REACH
    upper_taps = jnp.concatenate([upper[:, left + a : left + a + columns] for a in range(TAPS)])
    lower_taps = jnp.concatenate([lower[:, left + a : left + a + columns] for a in range(TAPS)])
    basis = (
        jnp.dot(high_ref[...], upper_taps, preferred_element_type=F32)
        + jnp.dot(high_ref[...], lower_taps, preferred_element_type=F32)
        + jnp.dot(low_ref[...], upper_taps, preferred_element_type=F32)
    )
    science = science_ref[...]
    place = iota((KP, columns), 0)
    for o in range(ROWS):
        image = basis[o * KP : (o + 1) * KP]
        image = jnp.where(place == BASIS, 1.0, image)
        image = jnp.where(place == UNKNOWNS, science[o : o + 1], image)
        design_ref[o] = image
        image_high, image_low = split(image)
        parts_ref[:KP, o * columns : (o + 1) * columns] = image_high
        parts_ref[KP:, o * columns : (o + 1) * columns] = image_low
    parts = parts_ref[...]
    gram = lax.dot_general(
        parts, parts, (((1,), (1,)), ((), ())), preferred_element_type=F32
    )
    half = gram[:KP] + gram[KP:]
    system = half[:, :KP] + half[:, KP:]
    down, across = iota((KP, KP), 0), iota((KP, KP), 1)
    diagonal = (down == across) & (down < UNKNOWNS)
    trace = jnp.sum(jnp.where(diagonal, system, 0.0))
    system = system + jnp.where(diagonal, RIDGE * trace / UNKNOWNS, 0.0)
    line = iota((KP, 1), 0)
    for k in range(UNKNOWNS):
        pivot = system[k : k + 1, :] * (1.0 / system[k : k + 1, k : k + 1])
        column = jnp.where(line == k, 0.0, system[:, k : k + 1])
        system = system - column * pivot
    scale = jnp.sum(jnp.where(diagonal, system, 0.0), axis=1, keepdims=True)
    fitted = jnp.where(
        line < UNKNOWNS, system[:, UNKNOWNS : UNKNOWNS + 1] / jnp.where(line < UNKNOWNS, scale, 1.0), 0.0
    )
    coefficients_ref[...] = jnp.sum(jnp.where(down == across, fitted, 0.0), axis=0, keepdims=True)[
        :, :UNKNOWNS
    ]
    for o in range(ROWS):
        model = jnp.sum(design_ref[o] * fitted, axis=0, keepdims=True)
        difference_ref[o : o + 1, :] = science[o : o + 1] - model


def call(kernel, outs, *args, scratch=()):
    return pl.pallas_call(
        kernel,
        out_shape=[jax.ShapeDtypeStruct(shape, dtype) for shape, dtype in outs],
        scratch_shapes=scratch,
        name=kernel.__name__,
    )(*args)


def body(strips, strip_patch, strip_row, strip_weight, science):
    peers = lax.axis_size("patch")
    count, lines, columns = strips.shape
    (payload,) = call(
        pack_kernel,
        [((peers * SLOTS, columns + EXTRA), BF16)],
        strips.reshape(count * lines, columns),
        strip_patch[None, :],
        strip_row[None, :],
        strip_weight.astype(F32)[None, :],
    )
    received = lax.all_to_all(
        payload.reshape(peers, SLOTS, columns + EXTRA), "patch", split_axis=0, concat_axis=0, tiled=True
    ).reshape(peers * SLOTS, columns + EXTRA)
    template, first, last = call(
        template_kernel,
        [((TROWS, columns), F32), ((TROWS, 128), F32), ((TROWS, 128), F32)],
        received,
    )
    devices = lax.axis_size("det")
    up = [(i, i + 1) for i in range(devices - 1)]
    before = lax.ppermute(last, "det", up)
    after = lax.ppermute(first, "det", [(j, i) for i, j in up])
    high, low = tap_table()
    difference, coefficients = call(
        fit_kernel,
        [((ROWS, columns), F32), ((1, UNKNOWNS), F32)],
        template,
        before,
        after,
        science[0],
        jnp.asarray(high),
        jnp.asarray(low),
        scratch=[
            pltpu.VMEM((ROWS, KP, columns), F32),
            pltpu.VMEM((2 * KP, ROWS * columns), BF16),
        ],
    )
    return (difference[None], coefficients[None])


def solution(mesh):
    placed = (P("patch", None, "det"), P("patch"), P("patch"), P("patch"), P("patch", None, "det"))
    return jax.shard_map(
        body,
        mesh=mesh,
        in_specs=placed,
        out_specs=(P("patch", None, "det"), P("patch", "det", None)),
        check_vma=False,
    )
```

time: 356 us -> 82.3 us (0.23)
  the two profiles are of different devices: /device:TPU:154 before, /device:TPU:10 now
where the time goes in v1:
time: 82.3 us; the launch traced here: 82 us
  blocking collectives  54.4 us (66%)
  Pallas kernels  14.1 us (17%)
  starting transfers between devices  5.83 us (7%)
  waiting for transfers between devices  3.38 us (4%)
  local copies, waits for them, and re-layouts  2.43 us (3%)
  other arithmetic  1.17 us (1%)
    all_to_all x1, blocking collectives, body(): lax.all_to_all(payload.reshape(peers, SLOTS, columns + EXTRA), 'patch', s...  54.4 us
    pallas_call x3, Pallas kernels, call(): pl.pallas_call(kernel, out_shape=[jax.ShapeDtypeStruct(shape, dtype) for...  14.1 us
    ppermute x1, starting transfers between devices, body(): before = lax.ppermute(last, 'det', up)  3.39 us
    ppermute x1, waiting for transfers between devices, body(): after = lax.ppermute(first, 'det', [(j, i) for i, j in up])  3.37 us
    ppermute x1, starting transfers between devices, body(): after = lax.ppermute(first, 'det', [(j, i) for i, j in up])  2.44 us
    reshape x1, local copies, waits for them, and re-layouts, body(): strips.reshape(count * lines, columns)  1.83 us
  transfers between devices with their start and end apart: 2, of which 1 were waited for; matrix products, arithmetic and copies ran while one was open for 0% of the time, Pallas kernels for 0%

profile of v1, /device:TPU:10, one launch (start us, length us, event | category | flops | bytes accessed | tf_op | source)
XLA Modules:
  0.0 82.0 jit_solution(11883627071394541926)
XLA Ops:
  0.6 1.2 %bitcast_convert_fusion.weight_ref = f32[1,96]{1,0:T(1,128)} fusion(bf16[96]{0:T(256)(128)(2,1)} %param.10), kind=kLoop, calls=%fused_computation | loop fusion | flops 96 | bytes 576 | tf_op jit(solution)/shard_map/broadcast_in_dim | solution.py:177
  1.8 1.8 %reshape.13.strips_ref = bf16[384,512]{1,0:T(8,128)(2,1)} reshape(bf16[96,4,512]{2,1,0:T(4,128)(2,1)} %param.7) | data formatting | bytes 786432 | tf_op jit(solution)/shard_map/reshape | solution.py:174
  3.6 3.2 %pack_kernel.1 = bf16[1024,640]{1,0:T(8,128)(2,1)} custom-call(bf16[384,512]{1,0:T(8,128)(2,1)} %reshape.13.strips_ref, s32[1,96]{1,0:T(1,128)} %bitcast.13, s32[1,96]{1,0:T(1,128)} %bitcast.14, f32[1,96]{1,0:T(1,128)} %bitcast_convert_fusion.weight_ref), custom_call_target="tpu_custom_call" | custom-call | tf_op jit(solution)/shard_map/pack_kernel/pallas_call | solution.py:160
  6.8 54.4 %all_to_all.5 = bf16[128,8,640]{2,1,0:T(8,128)(2,1)} all-to-all(bf16[128,8,640]{2,1,0:T(8,128)(2,1)} %bitcast.11), channel_id=1, replica_groups=mesh['patch'=128,'det'=4] {'patch'}, dimensions={0} | all-to-all | bytes 2621440 | tf_op jit(solution)/shard_map/all_to_all | solution.py:179
  61.3 2.4 %template_kernel.1 = (f32[32,512]{1,0:T(8,128)}, f32[32,128]{1,0:T(8,128)}, f32[32,128]{1,0:T(8,128)}) custom-call(bf16[1024,640]{1,0:T(8,128)(2,1)} %bitcast.10), custom_call_target="tpu_custom_call" | custom-call | tf_op jit(solution)/shard_map/template_kernel/pallas_call | solution.py:160
  63.7 3.4 %collective-permute-start = (f32[32,128]{1,0:T(8,128)}, f32[32,128]{1,0:T(8,128)S(1)}, u32[]{:S(2)}, u32[]{:S(2)}) collective-permute-start(f32[32,128]{1,0:T(8,128)} %get-tuple-element.8), channel_id=1, source_target_pairs={{0,1},{1,2},{2,3},{4,5},{5,6},{6,7},{8,9},{9,10},{10,11},{12,13},{... | collective-permute-start | bytes 49160 | tf_op jit(solution)/shard_map/ppermute | solution.py:189
  67.1 2.4 %collective-permute-start.1 = (f32[32,128]{1,0:T(8,128)}, f32[32,128]{1,0:T(8,128)S(1)}, u32[]{:S(2)}, u32[]{:S(2)}) collective-permute-start(f32[32,128]{1,0:T(8,128)} %get-tuple-element.9), channel_id=1, source_target_pairs={{1,0},{2,1},{3,2},{5,4},{6,5},{7,6},{9,8},{10,9},{11,10},{13,12},{... | collective-permute-start | bytes 49160 | tf_op jit(solution)/shard_map/ppermute | solution.py:190
  69.5 0.0 collective-permute-done.before_ref
  69.5 0.0 copy-start
  69.5 3.4 %collective-permute-done.1.after_ref = f32[32,128]{1,0:T(8,128)S(1)} collective-permute-done((f32[32,128]{1,0:T(8,128)}, f32[32,128]{1,0:T(8,128)S(1)}, u32[]{:S(2)}, u32[]{:S(2)}) %collective-permute-start.1) | collective-permute-done | bytes 16416 | tf_op jit(solution)/shard_map/ppermute | solution.py:190
  72.9 0.0 copy-start.1
  72.9 0.0 copy-done
  72.9 0.6 copy-done.1
  73.5 8.5 %fit_kernel.1 = (f32[8,512]{1,0:T(8,128)}, f32[1,46]{1,0:T(1,128)}) custom-call(f32[32,512]{1,0:T(8,128)} %get-tuple-element.7.template_ref, f32[32,128]{1,0:T(8,128)} %copy-done, f32[32,128]{1,0:T(8,128)} %copy-done.1, f32[8,512]{1,0:T(8,128)} %bitcast.12, bf16[384,672]{1,0:T(8,128)(2,1)} %constant.4.clone.high_ref, bf16[384,672]{1,0:T(8,128)(2,1)} %constant.5.clone.low_ref), custom_call_target="tpu_custom_call" | custom-call | tf_op jit(solution)/shard_map/fit_kernel/pallas_call | solution.py:160
Async XLA Ops:
  63.7 5.8 %collective-permute-start = (f32[32,128]{1,0:T(8,128)}, f32[32,128]{1,0:T(8,128)S(1)}, u32[]{:S(2)}, u32[]{:S(2)}) collective-permute-start(f32[32,128]{1,0:T(8,128)} %get-tuple-element.8), channel_id=1, source_target_pairs={{0,1},{1,2},{2,3},{4,5},{5,6},{6,7},{8,9},{9,10},{10,11},{12,13},{... | collective-permute-start | bytes 49160 | tf_op jit(solution)/shard_map/ppermute | solution.py:189
  67.1 5.8 %collective-permute-start.1 = (f32[32,128]{1,0:T(8,128)}, f32[32,128]{1,0:T(8,128)S(1)}, u32[]{:S(2)}, u32[]{:S(2)}) collective-permute-start(f32[32,128]{1,0:T(8,128)} %get-tuple-element.9), channel_id=1, source_target_pairs={{1,0},{2,1},{3,2},{5,4},{6,5},{7,6},{9,8},{10,9},{11,10},{13,12},{... | collective-permute-start | bytes 49160 | tf_op jit(solution)/shard_map/ppermute | solution.py:190
  69.5 3.4 %copy-start = (f32[32,128]{1,0:T(8,128)}, f32[32,128]{1,0:T(8,128)S(1)}, u32[]{:S(2)}) copy-start(f32[32,128]{1,0:T(8,128)S(1)} %collective-permute-done.before_ref) | copy-start | bytes 49156
  72.9 0.6 copy-start.1

commit v2 on v1

v2 whole, which is shorter than its diff:
```python
import jax
import jax.numpy as jnp
import numpy as np
from jax import lax
from jax.experimental import pallas as pl
from jax.experimental.pallas import tpu as pltpu
from jax.sharding import PartitionSpec as P

BASIS = 45
SIGMAS = (0.7, 1.5, 3.0)
RIDGE = 0.01
TAPS = 21
REACH = 10
ROWS = 8
TROWS = 32
SLOTS = 8
EXTRA = 128
SPREAD = 32
ONE = 64
KP = 48
UNKNOWNS = BASIS + 1
F32 = jnp.float32
BF16 = jnp.bfloat16


def tap_table():
    offsets = np.arange(TAPS, dtype=np.float64) - REACH
    profiles = []
    for width in SIGMAS:
        for degree in range(5):
            scaled = offsets / width
            profile = scaled**degree * np.exp(-0.5 * scaled * scaled)
            profiles.append(profile / np.sqrt(np.sum(profile * profile)))
    table = np.zeros((ROWS, KP, TAPS, TROWS))
    k = 0
    for s in range(3):
        for i in range(5):
            for j in range(5 - i):
                kernel = np.outer(profiles[5 * s + i], profiles[5 * s + j])
                for o in range(ROWS):
                    table[o, k, :, o : o + TAPS] = kernel
                k += 1
    table = table.reshape(ROWS * KP, TAPS * TROWS).astype(np.float32)
    high = table.astype(BF16)
    low = (table - high.astype(np.float32)).astype(BF16)
    return high, low


def iota(shape, dim):
    return lax.broadcasted_iota(jnp.int32, shape, dim)


def split(x):
    high = x.astype(BF16)
    return high, (x - high.astype(F32)).astype(BF16)


def pick_rows(key, base, step):
    shape = (step, key.shape[1])
    return (iota(shape, 0) + base == key).astype(F32).astype(BF16)


def pack_kernel(strips_ref, patch_ref, row_ref, weight_ref, out_ref, key_ref, extra_ref):
    count = patch_ref.shape[1]
    lines, columns = strips_ref.shape
    reps = lines // count
    first, second = iota((count, count), 0), iota((count, count), 1)
    patch = jnp.broadcast_to(patch_ref[...], (count, count))
    patch_col = jnp.sum(jnp.where(first == second, patch, 0).astype(F32), axis=1, keepdims=True)
    earlier = (patch.astype(F32) == patch_col) & (first < second)
    occurrence = jnp.sum(jnp.where(earlier, 1.0, 0.0), axis=0, keepdims=True)
    place = 2.0 * patch_ref[...].astype(F32) + occurrence
    spread = (iota((count, lines), 1) // reps == iota((count, lines), 0)).astype(F32).astype(BF16)
    wide = jnp.dot(
        jnp.broadcast_to(place, (8, count)).astype(BF16), spread, preferred_element_type=F32
    )[:1]
    key = wide.astype(jnp.int32) * reps + iota((1, lines), 1) % reps
    key_ref[...] = key
    strips = strips_ref[...]
    step = 256
    for base in range(0, out_ref.shape[0], step):
        out_ref[base : base + step, :] = jnp.dot(
            pick_rows(key, base, step), strips, preferred_element_type=F32
        ).astype(BF16)
    here = iota((lines, count), 0) // reps == iota((lines, count), 1)
    row = jnp.sum(
        jnp.where(here, row_ref[...].astype(F32), 0.0), axis=1, keepdims=True
    ).astype(jnp.int32)
    weight = jnp.sum(jnp.where(here, weight_ref[...].astype(F32), 0.0), axis=1, keepdims=True)
    lane = iota((lines, EXTRA), 1)
    at = row + iota((lines, EXTRA), 0) % reps + SPREAD
    extra_ref[...] = jnp.where(lane == at, weight, jnp.where(lane == ONE, 1.0, 0.0)).astype(BF16)


def edge_kernel(key_ref, extra_ref, before_ref, after_ref, unused_ref, out_ref):
    lane = iota(extra_ref.shape, 1)
    extra = jnp.where(
        lane < REACH,
        after_ref[...].astype(F32),
        jnp.where(lane >= EXTRA - REACH, before_ref[...].astype(F32), extra_ref[...].astype(F32)),
    ).astype(BF16)
    key = key_ref[...]
    step = 256
    for base in range(0, out_ref.shape[0], step):
        out_ref[base : base + step, :] = jnp.dot(
            pick_rows(key, base, step), extra, preferred_element_type=F32
        ).astype(BF16)


def fit_kernel(
    received_ref, science_ref, high_ref, low_ref,
    difference_ref, coefficients_ref, design_ref, parts_ref,
):
    columns = science_ref.shape[1]
    sums = lax.dot_general(
        received_ref[:, columns:],
        received_ref[...],
        (((0,), (0,)), ((), ())),
        preferred_element_type=F32,
    )[SPREAD : SPREAD + TROWS]
    coverage = sums[:, columns + ONE : columns + ONE + 1]
    template = sums / (1.0 + coverage)
    edges = template[:, columns:]
    upper, lower = split(jnp.concatenate([edges, template[:, :columns], edges], axis=1))
    left = EXTRA - REACH
    upper_taps = jnp.concatenate([upper[:, left + a : left + a + columns] for a in range(TAPS)])
    lower_taps = jnp.concatenate([lower[:, left + a : left + a + columns] for a in range(TAPS)])
    basis = (
        jnp.dot(high_ref[...], upper_taps, preferred_element_type=F32)
        + jnp.dot(high_ref[...], lower_taps, preferred_element_type=F32)
        + jnp.dot(low_ref[...], upper_taps, preferred_element_type=F32)
    )
    science = science_ref[...]
    place = iota((KP, columns), 0)
    for o in range(ROWS):
        image = basis[o * KP : (o + 1) * KP]
        image = jnp.where(place == BASIS, 1.0, image)
        image = jnp.where(place == UNKNOWNS, science[o : o + 1], image)
        design_ref[o] = image
        image_high, image_low = split(image)
        parts_ref[:KP, o * columns : (o + 1) * columns] = image_high
        parts_ref[KP:, o * columns : (o + 1) * columns] = image_low
    parts = parts_ref[...]
    gram = lax.dot_general(parts, parts, (((1,), (1,)), ((), ())), preferred_element_type=F32)
    half = gram[:KP] + gram[KP:]
    system = half[:, :KP] + half[:, KP:]
    down, across = iota((KP, KP), 0), iota((KP, KP), 1)
    diagonal = (down == across) & (down < UNKNOWNS)
    trace = jnp.sum(jnp.where(diagonal, system, 0.0))
    system = system + jnp.where(diagonal, RIDGE * trace / UNKNOWNS, 0.0)
    groups = [system[g : g + 8] for g in range(0, KP, 8)]
    line = iota((8, KP), 0)
    for k in range(0, UNKNOWNS, 2):
        at, own = k % 8, k // 8
        col0 = [jnp.broadcast_to(g[:, k : k + 1], (8, KP)) for g in groups]
        col1 = [jnp.broadcast_to(g[:, k + 1 : k + 2], (8, KP)) for g in groups]
        row0, row1 = groups[own][at : at + 1], groups[own][at + 1 : at + 2]
        a, b = col0[own][at : at + 1], col0[own][at + 1 : at + 2]
        d = col1[own][at + 1 : at + 2]
        inverse = 1.0 / (a * d - b * b)
        new0 = (d * row0 - b * row1) * inverse
        new1 = (a * row1 - b * row0) * inverse
        groups = [g - c0 * new0 - c1 * new1 for g, c0, c1 in zip(groups, col0, col1)]
        groups[own] = jnp.where(
            line == at, new0, jnp.where(line == at + 1, new1, groups[own])
        )
    system = jnp.concatenate(groups)
    fitted = jnp.where(down[:, :1] < UNKNOWNS, system[:, UNKNOWNS : UNKNOWNS + 1], 0.0)
    coefficients_ref[...] = jnp.sum(jnp.where(down == across, fitted, 0.0), axis=0, keepdims=True)[
        :, :UNKNOWNS
    ]
    for o in range(ROWS):
        model = jnp.sum(design_ref[o] * fitted, axis=0, keepdims=True)
        difference_ref[o : o + 1, :] = science[o : o + 1] - model


def call(kernel, outs, *args, **options):
    return pl.pallas_call(
        kernel,
        out_shape=[jax.ShapeDtypeStruct(shape, dtype) for shape, dtype in outs],
        name=kernel.__name__,
        **options,
    )(*args)


def pack(strips, strip_patch, strip_row, strip_weight, peers):
    lines, columns = strips.shape
    return call(
        pack_kernel,
        [
            ((peers * SLOTS, columns + EXTRA), BF16),
            ((1, lines), jnp.int32),
            ((lines, EXTRA), BF16),
        ],
        strips,
        strip_patch[None, :],
        strip_row[None, :],
        strip_weight[None, :],
        grid=(1,),
        out_specs=[
            pl.BlockSpec((peers * SLOTS, columns), lambda i: (0, 0)),
            pl.BlockSpec((1, lines), lambda i: (0, 0)),
            pl.BlockSpec((lines, EXTRA), lambda i: (0, 0)),
        ],
        cost_estimate=pl.CostEstimate(flops=10**9, bytes_accessed=2 * 10**6, transcendentals=0),
    )


def add_edges(payload, key, extra, before, after):
    rows, wide = payload.shape
    lines = key.shape[1]
    block = pl.BlockSpec((rows, EXTRA), lambda i: (0, wide // EXTRA - 1))
    whole = pl.BlockSpec((lines, EXTRA), lambda i: (0, 0))
    (payload,) = call(
        edge_kernel,
        [(payload.shape, BF16)],
        key,
        extra,
        before,
        after,
        payload,
        grid=(1,),
        in_specs=[pl.BlockSpec((1, lines), lambda i: (0, 0)), whole, whole, whole]
        + [pl.BlockSpec(memory_space=pl.ANY)],
        out_specs=[block],
        input_output_aliases={4: 0},
    )
    return payload


def fit(received, science):
    rows, columns = science.shape
    high, low = tap_table()
    return call(
        fit_kernel,
        [((rows, columns), F32), ((1, UNKNOWNS), F32)],
        received,
        science,
        jnp.asarray(high),
        jnp.asarray(low),
        scratch_shapes=[
            pltpu.VMEM((ROWS, KP, columns), F32),
            pltpu.VMEM((2 * KP, ROWS * columns), BF16),
        ],
    )


def body(strips, strip_patch, strip_row, strip_weight, science):
    peers = lax.axis_size("patch")
    devices = lax.axis_size("det")
    count, lines, columns = strips.shape
    up = [(i, i + 1) for i in range(devices - 1)]
    down = [(j, i) for i, j in up]
    last = strips[:, :, columns - EXTRA :].reshape(count * lines, EXTRA)
    first = strips[:, :, :EXTRA].reshape(count * lines, EXTRA)
    before = lax.ppermute(last, "det", up)
    after = lax.ppermute(first, "det", down)
    payload, key, extra = pack(
        strips.reshape(count * lines, columns), strip_patch, strip_row, strip_weight, peers
    )
    payload = add_edges(payload, key, extra, before, after)
    received = lax.all_to_all(
        payload.reshape(peers, SLOTS, columns + EXTRA),
        "patch",
        split_axis=0,
        concat_axis=0,
        tiled=True,
    ).reshape(peers * SLOTS, columns + EXTRA)
    difference, coefficients = fit(received, science[0])
    return (difference[None], coefficients[None])


def solution(mesh):
    placed = (P("patch", None, "det"), P("patch"), P("patch"), P("patch"), P("patch", None, "det"))
    return jax.shard_map(
        body,
        mesh=mesh,
        in_specs=placed,
        out_specs=(P("patch", None, "det"), P("patch", "det", None)),
        check_vma=False,
    )
```

time: 82.3 us -> 77.5 us (0.942)
  the two profiles are of different devices: /device:TPU:10 before, /device:TPU:1 now
where the time goes in v2:
time: 77.5 us; the launch traced here: 76.4 us
  blocking collectives  54.4 us (70%)
  Pallas kernels  12.6 us (16%)
  starting transfers between devices  5.23 us (7%)
  local copies, waits for them, and re-layouts  3.53 us (5%)
    all_to_all x1, blocking collectives, body(): lax.all_to_all(payload.reshape(peers, SLOTS, columns + EXTRA), 'patch', s...  54.4 us
    pallas_call x3, Pallas kernels, call(): pl.pallas_call(kernel, out_shape=[jax.ShapeDtypeStruct(shape, dtype) for...  12.6 us
    ppermute x1, starting transfers between devices, body(): before = lax.ppermute(last, 'det', up)  3.94 us
    reshape x1, local copies, waits for them, and re-layouts, body(): strips.reshape(count * lines, columns)  1.86 us
  transfers between devices with their start and end apart: 2, of which 0 were waited for; matrix products, arithmetic and copies ran while one was open for 2% of the time, Pallas kernels for 4%

profile of v2, /device:TPU:1, one launch (start us, length us, event | category | flops | bytes accessed | tf_op | source)
XLA Modules:
  0.0 76.4 jit_solution(2714120226843128504)
XLA Ops:
  0.6 1.0 %fusion = (bf16[96,4,128]{2,1,0:T(4,128)(2,1)S(1)}, bf16[96,4,128]{2,1,0:T(4,128)(2,1)S(1)}) fusion(bf16[96,4,512]{2,1,0:T(4,128)(2,1)} %param.7), kind=kLoop, calls=%fused_computation | loop fusion | bytes 393216 | tf_op jit(solution)/shard_map/slice | solution.py:255
  1.6 3.9 %collective-permute-start = (bf16[384,128]{1,0:T(8,128)(2,1)S(1)}, bf16[384,128]{1,0:T(8,128)(2,1)S(1)}, u32[]{:S(2)}, u32[]{:S(2)}) collective-permute-start(bf16[384,128]{1,0:T(8,128)(2,1)S(1)} %bitcast.13), channel_id=1, source_target_pairs={{0,1},{1,2},{2,3},{4,5},{5,6},{6,7},{8,9},{9,10},{10,11},{12,13},{... | collective-permute-start | bytes 294920 | tf_op jit(solution)/shard_map/ppermute | solution.py:256
  5.6 1.3 %collective-permute-start.1 = (bf16[384,128]{1,0:T(8,128)(2,1)S(1)}, bf16[384,128]{1,0:T(8,128)(2,1)S(1)}, u32[]{:S(2)}, u32[]{:S(2)}) collective-permute-start(bf16[384,128]{1,0:T(8,128)(2,1)S(1)} %bitcast.12), channel_id=1, source_target_pairs={{1,0},{2,1},{3,2},{5,4},{6,5},{7,6},{9,8},{10,9},{11,10},{13,12},{... | collective-permute-start | bytes 294920 | tf_op jit(solution)/shard_map/ppermute | solution.py:257
  6.9 1.9 %reshape.19.strips_ref = bf16[384,512]{1,0:T(8,128)(2,1)} reshape(bf16[96,4,512]{2,1,0:T(4,128)(2,1)} %param.7) | data formatting | bytes 786432 | tf_op jit(solution)/shard_map/reshape | solution.py:259
  8.7 3.0 %pack_kernel.1 = (bf16[1024,640]{1,0:T(8,128)(2,1)}, s32[1,384]{1,0:T(1,128)}, bf16[384,128]{1,0:T(8,128)(2,1)}) custom-call(bf16[384,512]{1,0:T(8,128)(2,1)} %reshape.19.strips_ref, s32[1,96]{1,0:T(1,128)} %bitcast.16, s32[1,96]{1,0:T(1,128)} %bitcast.17, bf16[1,96]{1,0:T(2,128)(2,1)} %bitcast.18), custom_call_target="tpu_custom_call" | custom-call | flops 1000000000 | bytes 2000000 | tf_op jit(solution)/shard_map/pack_kernel/pallas_call | solution.py:178
  11.7 0.0 collective-permute-done.before_ref
  11.7 0.0 copy-start
  11.7 0.0 collective-permute-done.1.after_ref
  11.7 0.0 copy-start.1
  11.7 0.6 copy-done
  12.4 0.0 copy-done.1
  12.4 2.1 %edge_kernel.1 = bf16[1024,640]{1,0:T(8,128)(2,1)} custom-call(s32[1,384]{1,0:T(1,128)} %get-tuple-element.7.key_ref, bf16[384,128]{1,0:T(8,128)(2,1)} %get-tuple-element.8.extra_ref, bf16[384,128]{1,0:T(8,128)(2,1)} %copy-done, bf16[384,128]{1,0:T(8,128)(2,1)} %copy-done.1, ...), custom_call_target="tpu_custom_call", output_to_operand_aliasing={{}: (4, {})} | custom-call | tf_op jit(solution)/shard_map/edge_kernel/pallas_call | solution.py:178
  14.5 54.4 %all_to_all.5 = bf16[128,8,640]{2,1,0:T(8,128)(2,1)} all-to-all(bf16[128,8,640]{2,1,0:T(8,128)(2,1)} %bitcast.10), channel_id=1, replica_groups=mesh['patch'=128,'det'=4] {'patch'}, dimensions={0} | all-to-all | bytes 2621440 | tf_op jit(solution)/shard_map/all_to_all | solution.py:262
  68.9 7.5 %fit_kernel.1 = (f32[8,512]{1,0:T(8,128)}, f32[1,46]{1,0:T(1,128)}) custom-call(bf16[1024,640]{1,0:T(8,128)(2,1)} %bitcast.11, f32[8,512]{1,0:T(8,128)} %bitcast.14, bf16[384,672]{1,0:T(8,128)(2,1)} %constant.4.clone.high_ref, bf16[384,672]{1,0:T(8,128)(2,1)} %constant.5.clone.low_ref), custom_call_target="tpu_custom_call" | custom-call | tf_op jit(solution)/shard_map/fit_kernel/pallas_call | solution.py:178
Async XLA Ops:
  1.6 10.1 %collective-permute-start = (bf16[384,128]{1,0:T(8,128)(2,1)S(1)}, bf16[384,128]{1,0:T(8,128)(2,1)S(1)}, u32[]{:S(2)}, u32[]{:S(2)}) collective-permute-start(bf16[384,128]{1,0:T(8,128)(2,1)S(1)} %bitcast.13), channel_id=1, source_target_pairs={{0,1},{1,2},{2,3},{4,5},{5,6},{6,7},{8,9},{9,10},{10,11},{12,13},{... | collective-permute-start | bytes 294920 | tf_op jit(solution)/shard_map/ppermute | solution.py:256
  5.6 6.1 %collective-permute-start.1 = (bf16[384,128]{1,0:T(8,128)(2,1)S(1)}, bf16[384,128]{1,0:T(8,128)(2,1)S(1)}, u32[]{:S(2)}, u32[]{:S(2)}) collective-permute-start(bf16[384,128]{1,0:T(8,128)(2,1)S(1)} %bitcast.12), channel_id=1, source_target_pairs={{1,0},{2,1},{3,2},{5,4},{6,5},{7,6},{9,8},{10,9},{11,10},{13,12},{... | collective-permute-start | bytes 294920 | tf_op jit(solution)/shard_map/ppermute | solution.py:257
  11.7 0.6 copy-start
  11.7 0.7 copy-start.1

commit v3 on v2

--- a/solution.py
+++ b/solution.py
@@ -19,6 +19,7 @@
 ONE = 64
 KP = 48
 UNKNOWNS = BASIS + 1
+VMEM_LIMIT = 12 * 2**20
 F32 = jnp.float32
 BF16 = jnp.bfloat16
 
@@ -60,16 +61,17 @@
     return (iota(shape, 0) + base == key).astype(F32).astype(BF16)
 
 
-def pack_kernel(strips_ref, patch_ref, row_ref, weight_ref, out_ref, key_ref, extra_ref):
-    count = patch_ref.shape[1]
+def pack_kernel(strips_ref, notes_ref, out_ref, key_ref, extra_ref):
+    count = notes_ref.shape[1]
+    patch_row, row_row, weight_row = (notes_ref[i : i + 1, :] for i in range(3))
     lines, columns = strips_ref.shape
     reps = lines // count
     first, second = iota((count, count), 0), iota((count, count), 1)
-    patch = jnp.broadcast_to(patch_ref[...], (count, count))
-    patch_col = jnp.sum(jnp.where(first == second, patch, 0).astype(F32), axis=1, keepdims=True)
-    earlier = (patch.astype(F32) == patch_col) & (first < second)
+    patch = jnp.broadcast_to(patch_row, (count, count))
+    patch_col = jnp.sum(jnp.where(first == second, patch, 0.0), axis=1, keepdims=True)
+    earlier = (patch == patch_col) & (first < second)
     occurrence = jnp.sum(jnp.where(earlier, 1.0, 0.0), axis=0, keepdims=True)
-    place = 2.0 * patch_ref[...].astype(F32) + occurrence
+    place = 2.0 * patch_row + occurrence
     spread = (iota((count, lines), 1) // reps == iota((count, lines), 0)).astype(F32).astype(BF16)
     wide = jnp.dot(
         jnp.broadcast_to(place, (8, count)).astype(BF16), spread, preferred_element_type=F32
@@ -83,10 +85,8 @@
             pick_rows(key, base, step), strips, preferred_element_type=F32
         ).astype(BF16)
     here = iota((lines, count), 0) // reps == iota((lines, count), 1)
-    row = jnp.sum(
-        jnp.where(here, row_ref[...].astype(F32), 0.0), axis=1, keepdims=True
-    ).astype(jnp.int32)
-    weight = jnp.sum(jnp.where(here, weight_ref[...].astype(F32), 0.0), axis=1, keepdims=True)
+    row = jnp.sum(jnp.where(here, row_row, 0.0), axis=1, keepdims=True).astype(jnp.int32)
+    weight = jnp.sum(jnp.where(here, weight_row, 0.0), axis=1, keepdims=True)
     lane = iota((lines, EXTRA), 1)
     at = row + iota((lines, EXTRA), 0) % reps + SPREAD
     extra_ref[...] = jnp.where(lane == at, weight, jnp.where(lane == ONE, 1.0, 0.0)).astype(BF16)
@@ -179,12 +179,14 @@
         kernel,
         out_shape=[jax.ShapeDtypeStruct(shape, dtype) for shape, dtype in outs],
         name=kernel.__name__,
+        compiler_params=pltpu.CompilerParams(vmem_limit_bytes=VMEM_LIMIT),
         **options,
     )(*args)
 
 
 def pack(strips, strip_patch, strip_row, strip_weight, peers):
     lines, columns = strips.shape
+    notes = jnp.stack([x.astype(F32) for x in (strip_patch, strip_row, strip_weight)])
     return call(
         pack_kernel,
         [
@@ -193,9 +195,7 @@
             ((lines, EXTRA), BF16),
         ],
         strips,
-        strip_patch[None, :],
-        strip_row[None, :],
-        strip_weight[None, :],
+        notes,
         grid=(1,),
         out_specs=[
             pl.BlockSpec((peers * SLOTS, columns), lambda i: (0, 0)),

time: 77.5 us -> 72.6 us (0.937); the launches traced: 76.4 us -> 72.3 us
  Pallas kernels: 12.6 us -> 7.23 us
  local copies, waits for them, and re-layouts: 3.53 us -> 2.12 us
  other arithmetic: 0 us -> 1.35 us
    pallas_call x3, Pallas kernels: 12.6 us -> 7.23 us  [call(): pl.pallas_call(kernel, out_shape=[jax.ShapeDtypeStruct(shape, dtype) for...]
    another operation x0 -> x3, other arithmetic: none -> 1.35 us  [pack(): jnp.stack([x.astype(F32) for x in (strip_patch, strip_row, strip_weight)])]
  transfers between devices with their start and end apart: 2 -> 2, of which waited for: 0 -> 1; matrix products, arithmetic and copies ran while one was open for 2% -> 3% of each run, Pallas kernels for 4% -> 1%
where the time goes in v3:
time: 72.6 us; the launch traced here: 72.3 us
  blocking collectives  55 us (76%)
  Pallas kernels  7.23 us (10%)
  starting transfers between devices  5.23 us (7%)
  local copies, waits for them, and re-layouts  2.12 us (3%)
  other arithmetic  1.35 us (2%)
    all_to_all x1, blocking collectives, body(): lax.all_to_all(payload.reshape(peers, SLOTS, columns + EXTRA), 'patch', s...  55 us
    pallas_call x3, Pallas kernels, call(): pl.pallas_call(kernel, out_shape=[jax.ShapeDtypeStruct(shape, dtype) for...  7.23 us
    ppermute x1, starting transfers between devices, body(): before = lax.ppermute(last, 'det', up)  3.94 us
  transfers between devices with their start and end apart: 2, of which 1 were waited for; matrix products, arithmetic and copies ran while one was open for 3% of the time, Pallas kernels for 1%

profile of v3, /device:TPU:1, one launch (start us, length us, event | category | flops | bytes accessed | tf_op | source)
XLA Modules:
  0.0 72.3 jit_solution(4971155165650516654)
XLA Ops:
  0.6 1.0 %fusion = (bf16[96,4,128]{2,1,0:T(4,128)(2,1)S(1)}, bf16[96,4,128]{2,1,0:T(4,128)(2,1)S(1)}) fusion(bf16[96,4,512]{2,1,0:T(4,128)(2,1)} %param.7), kind=kLoop, calls=%fused_computation.4 | loop fusion | bytes 393216 | tf_op jit(solution)/shard_map/slice | solution.py:255
  1.6 3.9 %collective-permute-start = (bf16[384,128]{1,0:T(8,128)(2,1)S(1)}, bf16[384,128]{1,0:T(8,128)(2,1)S(1)}, u32[]{:S(2)}, u32[]{:S(2)}) collective-permute-start(bf16[384,128]{1,0:T(8,128)(2,1)S(1)} %bitcast.18), channel_id=1, source_target_pairs={{0,1},{1,2},{2,3},{4,5},{5,6},{6,7},{8,9},{9,10},{10,11},{12,13},{... | collective-permute-start | bytes 294920 | tf_op jit(solution)/shard_map/ppermute | solution.py:256
  5.6 1.3 %collective-permute-start.1 = (bf16[384,128]{1,0:T(8,128)(2,1)S(1)}, bf16[384,128]{1,0:T(8,128)(2,1)S(1)}, u32[]{:S(2)}, u32[]{:S(2)}) collective-permute-start(bf16[384,128]{1,0:T(8,128)(2,1)S(1)} %bitcast.17), channel_id=1, source_target_pairs={{1,0},{2,1},{3,2},{5,4},{6,5},{7,6},{9,8},{10,9},{11,10},{13,12},{... | collective-permute-start | bytes 294920 | tf_op jit(solution)/shard_map/ppermute | solution.py:257
  6.9 0.7 bitcast_convert_fusion
  7.6 0.7 convert_bitcast_fusion
  8.2 1.1 %reshape.19.strips_ref = bf16[384,512]{1,0:T(8,128)(2,1)S(1)} reshape(bf16[96,4,512]{2,1,0:T(4,128)(2,1)} %param.7) | data formatting | bytes 786432 | tf_op jit(solution)/shard_map/reshape | solution.py:259
  9.3 0.9 %pack_kernel.1 = (bf16[1024,640]{1,0:T(8,128)(2,1)S(1)}, s32[1,384]{1,0:T(1,128)S(1)}, bf16[384,128]{1,0:T(8,128)(2,1)S(1)}) custom-call(bf16[384,512]{1,0:T(8,128)(2,1)S(1)} %reshape.19.strips_ref, f32[3,96]{1,0:T(4,128)S(1)} %pad_maximum_fusion.notes_ref), custom_call_target="tpu_custom_call" | custom-call | flops 1000000000 | bytes 2000000 | tf_op jit(solution)/shard_map/pack_kernel/pallas_call | solution.py:178
  10.2 0.0 collective-permute-done.before_ref
  10.3 0.7 collective-permute-done.1.after_ref
  11.0 0.4 edge_kernel.1
  11.4 0.0 copy-start
  11.4 0.0 copy-start.1
  11.4 0.0 copy-start.2
  11.4 55.0 %all_to_all.5 = bf16[128,8,640]{2,1,0:T(8,128)(2,1)S(1)} all-to-all(bf16[128,8,640]{2,1,0:T(8,128)(2,1)S(1)} %bitcast.14), channel_id=1, replica_groups=mesh['patch'=128,'det'=4] {'patch'}, dimensions={0} | all-to-all | bytes 2621440 | tf_op jit(solution)/shard_map/all_to_all | solution.py:262
  66.4 0.0 copy-done
  66.4 0.0 copy-done.1
  66.4 0.0 copy-done.2
  66.5 5.9 %fit_kernel.1 = (f32[8,512]{1,0:T(8,128)}, f32[1,46]{1,0:T(1,128)}) custom-call(bf16[1024,640]{1,0:T(8,128)(2,1)S(1)} %bitcast.15, f32[8,512]{1,0:T(8,128)S(1)} %bitcast.16, bf16[384,672]{1,0:T(8,128)(2,1)S(1)} %copy-done.1, bf16[384,672]{1,0:T(8,128)(2,1)S(1)} %copy-done), custom_call_target="tpu_custom_call" | custom-call | tf_op jit(solution)/shard_map/fit_kernel/pallas_call | solution.py:178
  (1 shorter events, 0.0 us)
Async XLA Ops:
  1.6 8.6 %collective-permute-start = (bf16[384,128]{1,0:T(8,128)(2,1)S(1)}, bf16[384,128]{1,0:T(8,128)(2,1)S(1)}, u32[]{:S(2)}, u32[]{:S(2)}) collective-permute-start(bf16[384,128]{1,0:T(8,128)(2,1)S(1)} %bitcast.18), channel_id=1, source_target_pairs={{0,1},{1,2},{2,3},{4,5},{5,6},{6,7},{8,9},{9,10},{10,11},{12,13},{... | collective-permute-start | bytes 294920 | tf_op jit(solution)/shard_map/ppermute | solution.py:256
  5.6 5.4 %collective-permute-start.1 = (bf16[384,128]{1,0:T(8,128)(2,1)S(1)}, bf16[384,128]{1,0:T(8,128)(2,1)S(1)}, u32[]{:S(2)}, u32[]{:S(2)}) collective-permute-start(bf16[384,128]{1,0:T(8,128)(2,1)S(1)} %bitcast.17), channel_id=1, source_target_pairs={{1,0},{2,1},{3,2},{5,4},{6,5},{7,6},{9,8},{10,9},{11,10},{13,12},{... | collective-permute-start | bytes 294920 | tf_op jit(solution)/shard_map/ppermute | solution.py:257
  11.4 55.0 %copy-start = (bf16[384,672]{1,0:T(8,128)(2,1)S(1)}, bf16[384,672]{1,0:T(8,128)(2,1)}, u32[]{:S(2)}) copy-start(bf16[384,672]{1,0:T(8,128)(2,1)} %constant.5.clone.low_ref) | copy-start | bytes 1548292
  11.4 55.0 %copy-start.1 = (bf16[384,672]{1,0:T(8,128)(2,1)S(1)}, bf16[384,672]{1,0:T(8,128)(2,1)}, u32[]{:S(2)}) copy-start(bf16[384,672]{1,0:T(8,128)(2,1)} %constant.4.clone.high_ref) | copy-start | bytes 1548292
  11.4 55.0 %copy-start.2 = (f32[1,8,512]{2,1,0:T(8,128)S(1)}, f32[1,8,512]{2,1,0:T(8,128)}, u32[]{:S(2)}) copy-start(f32[1,8,512]{2,1,0:T(8,128)} %param.11) | copy-start | bytes 49156

commit v4 on v3

--- a/solution.py
+++ b/solution.py
@@ -44,7 +44,7 @@
     table = table.reshape(ROWS * KP, TAPS * TROWS).astype(np.float32)
     high = table.astype(BF16)
     low = (table - high.astype(np.float32)).astype(BF16)
-    return high, low
+    return np.concatenate([high, high, low], axis=1)
 
 
 def iota(shape, dim):
@@ -107,8 +107,42 @@
         ).astype(BF16)
 
 
+def invert_pair(a, b, d):
+    inverse = 1.0 / (a * d - b * b)
+    return d * inverse, -b * inverse, a * inverse
+
+
+def solve_block(m, rows):
+    a, b, d = invert_pair(m[0][0], m[0][1], m[1][1])
+    first = [a * rows[0] + b * rows[1], b * rows[0] + d * rows[1]]
+    if len(rows) == 2:
+        return first
+    w = [[a * m[0][j] + b * m[1][j] for j in (2, 3)], [b * m[0][j] + d * m[1][j] for j in (2, 3)]]
+    s = [[m[2 + i][2 + j] - m[0][2 + i] * w[0][j] - m[1][2 + i] * w[1][j] for j in (0, 1)] for i in (0, 1)]
+    a, b, d = invert_pair(s[0][0], s[0][1], s[1][1])
+    rest = [rows[2 + i] - m[0][2 + i] * first[0] - m[1][2 + i] * first[1] for i in (0, 1)]
+    last = [a * rest[0] + b * rest[1], b * rest[0] + d * rest[1]]
+    return [first[i] - w[i][0] * last[0] - w[i][1] * last[1] for i in (0, 1)] + last
+
+
+def spread_columns(groups, k):
+    return [
+        [jnp.broadcast_to(g[:, j : j + 1], g.shape) for g in groups]
+        for j in range(k, min(k + 4, UNKNOWNS))
+    ]
+
+
+def eliminate(groups, block, spread, own, at, line):
+    new = solve_block(block, [groups[own][at + i : at + i + 1] for i in range(len(spread))])
+    for column, row in zip(spread, new):
+        groups = [g - c * row for g, c in zip(groups, column)]
+    for i, row in enumerate(new):
+        groups[own] = jnp.where(line == at + i, row, groups[own])
+    return groups
+
+
 def fit_kernel(
-    received_ref, science_ref, high_ref, low_ref,
+    received_ref, science_ref, table_ref,
     difference_ref, coefficients_ref, design_ref, parts_ref,
 ):
     columns = science_ref.shape[1]
@@ -125,17 +159,18 @@
     left = EXTRA - REACH
     upper_taps = jnp.concatenate([upper[:, left + a : left + a + columns] for a in range(TAPS)])
     lower_taps = jnp.concatenate([lower[:, left + a : left + a + columns] for a in range(TAPS)])
-    basis = (
-        jnp.dot(high_ref[...], upper_taps, preferred_element_type=F32)
-        + jnp.dot(high_ref[...], lower_taps, preferred_element_type=F32)
-        + jnp.dot(low_ref[...], upper_taps, preferred_element_type=F32)
+    basis = jnp.dot(
+        table_ref[...],
+        jnp.concatenate([upper_taps, lower_taps, upper_taps]),
+        preferred_element_type=F32,
     )
     science = science_ref[...]
-    place = iota((KP, columns), 0)
+    place = iota((8, columns), 0)
     for o in range(ROWS):
         image = basis[o * KP : (o + 1) * KP]
-        image = jnp.where(place == BASIS, 1.0, image)
-        image = jnp.where(place == UNKNOWNS, science[o : o + 1], image)
+        tail = jnp.where(place == BASIS - KP + 8, 1.0, image[KP - 8 :])
+        tail = jnp.where(place == UNKNOWNS - KP + 8, science[o : o + 1], tail)
+        image = jnp.concatenate([image[: KP - 8], tail])
         design_ref[o] = image
         image_high, image_low = split(image)
         parts_ref[:KP, o * columns : (o + 1) * columns] = image_high
@@ -150,20 +185,13 @@
     system = system + jnp.where(diagonal, RIDGE * trace / UNKNOWNS, 0.0)
     groups = [system[g : g + 8] for g in range(0, KP, 8)]
     line = iota((8, KP), 0)
-    for k in range(0, UNKNOWNS, 2):
-        at, own = k % 8, k // 8
-        col0 = [jnp.broadcast_to(g[:, k : k + 1], (8, KP)) for g in groups]
-        col1 = [jnp.broadcast_to(g[:, k + 1 : k + 2], (8, KP)) for g in groups]
-        row0, row1 = groups[own][at : at + 1], groups[own][at + 1 : at + 2]
-        a, b = col0[own][at : at + 1], col0[own][at + 1 : at + 2]
-        d = col1[own][at + 1 : at + 2]
-        inverse = 1.0 / (a * d - b * b)
-        new0 = (d * row0 - b * row1) * inverse
-        new1 = (a * row1 - b * row0) * inverse
-        groups = [g - c0 * new0 - c1 * new1 for g, c0, c1 in zip(groups, col0, col1)]
-        groups[own] = jnp.where(
-            line == at, new0, jnp.where(line == at + 1, new1, groups[own])
-        )
+    spread = spread_columns(groups, 0)
+    for k in range(0, UNKNOWNS, 4):
+        at, own, size = k % 8, k // 8, len(spread)
+        ahead = spread_columns(groups, k + 4)
+        block = [[c[own][at + i : at + i + 1] for c in spread] for i in range(size)]
+        groups = eliminate(groups, block, spread, own, at, line)
+        spread = [eliminate(c, block, spread, own, at, line) for c in ahead]
     system = jnp.concatenate(groups)
     fitted = jnp.where(down[:, :1] < UNKNOWNS, system[:, UNKNOWNS : UNKNOWNS + 1], 0.0)
     coefficients_ref[...] = jnp.sum(jnp.where(down == across, fitted, 0.0), axis=0, keepdims=True)[
@@ -230,14 +258,12 @@
 
 def fit(received, science):
     rows, columns = science.shape
-    high, low = tap_table()
     return call(
         fit_kernel,
         [((rows, columns), F32), ((1, UNKNOWNS), F32)],
         received,
         science,
-        jnp.asarray(high),
-        jnp.asarray(low),
+        jnp.asarray(tap_table()),
         scratch_shapes=[
             pltpu.VMEM((ROWS, KP, columns), F32),
             pltpu.VMEM((2 * KP, ROWS * columns), BF16),

time: 72.6 us -> 71.3 us (0.982)
  Pallas kernels: 7.23 us -> 6 us
    pallas_call x3, Pallas kernels: 7.23 us -> 6 us  [call(): pl.pallas_call(kernel, out_shape=[jax.ShapeDtypeStruct(shape, dtype) for...]
where the time goes in v4:
time: 71.3 us; the launch traced here: 71.1 us
  blocking collectives  55 us (77%)
  Pallas kernels  6 us (8%)
  starting transfers between devices  5.23 us (7%)
  local copies, waits for them, and re-layouts  2.12 us (3%)
  other arithmetic  1.35 us (2%)
    all_to_all x1, blocking collectives, body(): lax.all_to_all(payload.reshape(peers, SLOTS, columns + EXTRA), 'patch', s...  55 us
    pallas_call x3, Pallas kernels, call(): pl.pallas_call(kernel, out_shape=[jax.ShapeDtypeStruct(shape, dtype) for...  6 us
    ppermute x1, starting transfers between devices, body(): before = lax.ppermute(last, 'det', up)  3.94 us
  transfers between devices with their start and end apart: 2, of which 1 were waited for; matrix products, arithmetic and copies ran while one was open for 3% of the time, Pallas kernels for 1%

profile of v4, /device:TPU:1, one launch (start us, length us, event | category | flops | bytes accessed | tf_op | source)
XLA Modules:
  0.0 71.1 jit_solution(9987559387096706784)
XLA Ops:
  0.6 1.0 %fusion = (bf16[96,4,128]{2,1,0:T(4,128)(2,1)S(1)}, bf16[96,4,128]{2,1,0:T(4,128)(2,1)S(1)}) fusion(bf16[96,4,512]{2,1,0:T(4,128)(2,1)} %param.6), kind=kLoop, calls=%fused_computation.4 | loop fusion | bytes 393216 | tf_op jit(solution)/shard_map/slice | solution.py:281
  1.6 3.9 %collective-permute-start = (bf16[384,128]{1,0:T(8,128)(2,1)S(1)}, bf16[384,128]{1,0:T(8,128)(2,1)S(1)}, u32[]{:S(2)}, u32[]{:S(2)}) collective-permute-start(bf16[384,128]{1,0:T(8,128)(2,1)S(1)} %bitcast.18), channel_id=1, source_target_pairs={{0,1},{1,2},{2,3},{4,5},{5,6},{6,7},{8,9},{9,10},{10,11},{12,13},{... | collective-permute-start | bytes 294920 | tf_op jit(solution)/shard_map/ppermute | solution.py:282
  5.6 1.3 %collective-permute-start.1 = (bf16[384,128]{1,0:T(8,128)(2,1)S(1)}, bf16[384,128]{1,0:T(8,128)(2,1)S(1)}, u32[]{:S(2)}, u32[]{:S(2)}) collective-permute-start(bf16[384,128]{1,0:T(8,128)(2,1)S(1)} %bitcast.17), channel_id=1, source_target_pairs={{1,0},{2,1},{3,2},{5,4},{6,5},{7,6},{9,8},{10,9},{11,10},{13,12},{... | collective-permute-start | bytes 294920 | tf_op jit(solution)/shard_map/ppermute | solution.py:283
  6.9 0.7 bitcast_convert_fusion
  7.6 0.7 convert_bitcast_fusion
  8.2 1.1 %reshape.19.strips_ref = bf16[384,512]{1,0:T(8,128)(2,1)S(1)} reshape(bf16[96,4,512]{2,1,0:T(4,128)(2,1)} %param.6) | data formatting | bytes 786432 | tf_op jit(solution)/shard_map/reshape | solution.py:285
  9.3 0.9 %pack_kernel.1 = (bf16[1024,640]{1,0:T(8,128)(2,1)S(1)}, s32[1,384]{1,0:T(1,128)S(1)}, bf16[384,128]{1,0:T(8,128)(2,1)S(1)}) custom-call(bf16[384,512]{1,0:T(8,128)(2,1)S(1)} %reshape.19.strips_ref, f32[3,96]{1,0:T(4,128)S(1)} %pad_maximum_fusion.notes_ref), custom_call_target="tpu_custom_call" | custom-call | flops 1000000000 | bytes 2000000 | tf_op jit(solution)/shard_map/pack_kernel/pallas_call | solution.py:206
  10.2 0.0 collective-permute-done.before_ref
  10.3 0.7 collective-permute-done.1.after_ref
  11.0 0.4 edge_kernel.1
  11.4 0.0 copy-start
  11.4 0.0 copy-start.1
  11.4 55.0 %all_to_all.5 = bf16[128,8,640]{2,1,0:T(8,128)(2,1)S(1)} all-to-all(bf16[128,8,640]{2,1,0:T(8,128)(2,1)S(1)} %bitcast.14), channel_id=1, replica_groups=mesh['patch'=128,'det'=4] {'patch'}, dimensions={0} | all-to-all | bytes 2621440 | tf_op jit(solution)/shard_map/all_to_all | solution.py:288
  66.4 0.0 copy-done
  66.4 0.0 copy-done.1
  66.4 4.6 %fit_kernel.1 = (f32[8,512]{1,0:T(8,128)}, f32[1,46]{1,0:T(1,128)}) custom-call(bf16[1024,640]{1,0:T(8,128)(2,1)S(1)} %bitcast.15, f32[8,512]{1,0:T(8,128)S(1)} %bitcast.16, bf16[384,2016]{1,0:T(8,128)(2,1)S(1)} %copy-done), custom_call_target="tpu_custom_call" | custom-call | tf_op jit(solution)/shard_map/fit_kernel/pallas_call | solution.py:206
  (1 shorter events, 0.0 us)
Async XLA Ops:
  1.6 8.6 %collective-permute-start = (bf16[384,128]{1,0:T(8,128)(2,1)S(1)}, bf16[384,128]{1,0:T(8,128)(2,1)S(1)}, u32[]{:S(2)}, u32[]{:S(2)}) collective-permute-start(bf16[384,128]{1,0:T(8,128)(2,1)S(1)} %bitcast.18), channel_id=1, source_target_pairs={{0,1},{1,2},{2,3},{4,5},{5,6},{6,7},{8,9},{9,10},{10,11},{12,13},{... | collective-permute-start | bytes 294920 | tf_op jit(solution)/shard_map/ppermute | solution.py:282
  5.6 5.4 %collective-permute-start.1 = (bf16[384,128]{1,0:T(8,128)(2,1)S(1)}, bf16[384,128]{1,0:T(8,128)(2,1)S(1)}, u32[]{:S(2)}, u32[]{:S(2)}) collective-permute-start(bf16[384,128]{1,0:T(8,128)(2,1)S(1)} %bitcast.17), channel_id=1, source_target_pairs={{1,0},{2,1},{3,2},{5,4},{6,5},{7,6},{9,8},{10,9},{11,10},{13,12},{... | collective-permute-start | bytes 294920 | tf_op jit(solution)/shard_map/ppermute | solution.py:283
  11.4 55.0 %copy-start = (bf16[384,2016]{1,0:T(8,128)(2,1)S(1)}, bf16[384,2016]{1,0:T(8,128)(2,1)}, u32[]{:S(2)}) copy-start(bf16[384,2016]{1,0:T(8,128)(2,1)} %constant.2.clone.table_ref) | copy-start | bytes 4644868
  11.4 55.0 %copy-start.1 = (f32[1,8,512]{2,1,0:T(8,128)S(1)}, f32[1,8,512]{2,1,0:T(8,128)}, u32[]{:S(2)}) copy-start(f32[1,8,512]{2,1,0:T(8,128)} %param.10) | copy-start | bytes 49156

commit v5 on v4

--- a/solution.py
+++ b/solution.py
@@ -13,10 +13,13 @@
 REACH = 10
 ROWS = 8
 TROWS = 32
-SLOTS = 8
-EXTRA = 128
-SPREAD = 32
-ONE = 64
+LANES = 128
+TILES = 9
+NOTES = 4
+HALF = 64
+EDGE = 32
+ONE = 52
+TURN = 86
 KP = 48
 UNKNOWNS = BASIS + 1
 VMEM_LIMIT = 12 * 2**20
@@ -61,50 +64,65 @@
     return (iota(shape, 0) + base == key).astype(F32).astype(BF16)
 
 
-def pack_kernel(strips_ref, notes_ref, out_ref, key_ref, extra_ref):
-    count = notes_ref.shape[1]
-    patch_row, row_row, weight_row = (notes_ref[i : i + 1, :] for i in range(3))
+def pack_kernel(strips_ref, about_ref, out_ref, key_ref, notes_ref, second_ref):
+    count = about_ref.shape[1]
+    patch_row, row_row, weight_row = (about_ref[i : i + 1, :] for i in range(3))
     lines, columns = strips_ref.shape
     reps = lines // count
     first, second = iota((count, count), 0), iota((count, count), 1)
     patch = jnp.broadcast_to(patch_row, (count, count))
     patch_col = jnp.sum(jnp.where(first == second, patch, 0.0), axis=1, keepdims=True)
     earlier = (patch == patch_col) & (first < second)
-    occurrence = jnp.sum(jnp.where(earlier, 1.0, 0.0), axis=0, keepdims=True)
-    place = 2.0 * patch_row + occurrence
+    slot = jnp.sum(jnp.where(earlier, 1.0, 0.0), axis=0, keepdims=True)
     spread = (iota((count, lines), 1) // reps == iota((count, lines), 0)).astype(F32).astype(BF16)
     wide = jnp.dot(
-        jnp.broadcast_to(place, (8, count)).astype(BF16), spread, preferred_element_type=F32
-    )[:1]
-    key = wide.astype(jnp.int32) * reps + iota((1, lines), 1) % reps
-    key_ref[...] = key
+        jnp.where(iota((8, count), 0) == 0, 2.0 * patch_row + slot, patch_row).astype(BF16),
+        spread,
+        preferred_element_type=F32,
+    ).astype(jnp.int32) * reps + iota((8, lines), 1) % reps
+    key = wide[:1]
+    key_ref[...] = wide[1:2]
     strips = strips_ref[...]
     step = 256
-    for base in range(0, out_ref.shape[0], step):
-        out_ref[base : base + step, :] = jnp.dot(
-            pick_rows(key, base, step), strips, preferred_element_type=F32
-        ).astype(BF16)
+    pairs = step // 16
+    for i in range(out_ref.shape[0] // pairs):
+        picked = jnp.dot(pick_rows(key, i * step, step), strips, preferred_element_type=F32)
+        picked = picked.reshape(pairs, 2, 8, columns)
+        for c in range(columns // LANES):
+            for odd in range(2):
+                out_ref[i * pairs : (i + 1) * pairs, c + odd * (NOTES + 1)] = picked[
+                    :, odd, :, c * LANES : (c + 1) * LANES
+                ].astype(BF16)
     here = iota((lines, count), 0) // reps == iota((lines, count), 1)
-    row = jnp.sum(jnp.where(here, row_row, 0.0), axis=1, keepdims=True).astype(jnp.int32)
-    weight = jnp.sum(jnp.where(here, weight_row, 0.0), axis=1, keepdims=True)
-    lane = iota((lines, EXTRA), 1)
-    at = row + iota((lines, EXTRA), 0) % reps + SPREAD
-    extra_ref[...] = jnp.where(lane == at, weight, jnp.where(lane == ONE, 1.0, 0.0)).astype(BF16)
-
-
-def edge_kernel(key_ref, extra_ref, before_ref, after_ref, unused_ref, out_ref):
-    lane = iota(extra_ref.shape, 1)
-    extra = jnp.where(
+
+    def line_of(values):
+        return jnp.sum(jnp.where(here, values, 0.0), axis=1, keepdims=True)
+
+    lane = iota((lines, LANES), 1)
+    start = line_of(slot).astype(jnp.int32) * HALF
+    at = start + line_of(row_row).astype(jnp.int32) + iota((lines, LANES), 0) % reps
+    notes_ref[...] = jnp.where(
+        lane == at, line_of(weight_row), jnp.where(lane == start + ONE, 1.0, 0.0)
+    ).astype(BF16)
+    second_ref[...] = jnp.broadcast_to(line_of(slot), (lines, LANES)).astype(BF16)
+
+
+def notes_kernel(key_ref, notes_ref, second_ref, before_ref, after_ref, unused_ref, out_ref):
+    lane = iota(notes_ref.shape, 1)
+    edges = jnp.where(
         lane < REACH,
         after_ref[...].astype(F32),
-        jnp.where(lane >= EXTRA - REACH, before_ref[...].astype(F32), extra_ref[...].astype(F32)),
-    ).astype(BF16)
+        jnp.where(lane >= LANES - REACH, before_ref[...].astype(F32), 0.0),
+    )
+    edges = pltpu.roll(edges, LANES - TURN, 1)
+    edges = jnp.where(second_ref[...].astype(F32) > 0.5, pltpu.roll(edges, HALF, 1), edges)
+    notes = (notes_ref[...].astype(F32) + edges).astype(BF16)
     key = key_ref[...]
     step = 256
-    for base in range(0, out_ref.shape[0], step):
-        out_ref[base : base + step, :] = jnp.dot(
-            pick_rows(key, base, step), extra, preferred_element_type=F32
-        ).astype(BF16)
+    pairs = step // 8
+    for i in range(out_ref.shape[0] // pairs):
+        picked = jnp.dot(pick_rows(key, i * step, step), notes, preferred_element_type=F32)
+        out_ref[i * pairs : (i + 1) * pairs, 0] = picked.reshape(pairs, 8, LANES).astype(BF16)
 
 
 def invert_pair(a, b, d):
@@ -142,21 +160,50 @@
 
 
 def fit_kernel(
-    received_ref, science_ref, table_ref,
+    odd_ref, received_ref, science_ref, table_ref,
     difference_ref, coefficients_ref, design_ref, parts_ref,
 ):
     columns = science_ref.shape[1]
+    odd = odd_ref[0]
+
+    def tile(i):
+        return received_ref[:, i].astype(F32)
+
+    low = iota((received_ref.shape[0], 8, LANES), 1) < 4
+    whole, off = (NOTES + 1) * odd, NOTES * (1 - odd)
+    parts = [
+        jnp.concatenate([tile(whole + c), jnp.where(low, tile(off + 1 + c), tile(off + c))])
+        for c in range(columns // LANES)
+    ]
+    mine, other = tile(NOTES), tile(2 * off)
+    mine_turned, other_turned = pltpu.roll(mine, 4, 1), pltpu.roll(other, 4, 1)
+    mine, mine_turned = (
+        jnp.where(odd == 1, mine_turned, mine),
+        jnp.where(odd == 1, mine, mine_turned),
+    )
+    other, other_turned = (
+        jnp.where(odd == 1, other_turned, other),
+        jnp.where(odd == 1, other, other_turned),
+    )
+    spread = jnp.concatenate(
+        [
+            jnp.where(low, mine, pltpu.roll(mine_turned, HALF, 2)),
+            jnp.where(low, pltpu.roll(other_turned, HALF, 2), other),
+        ]
+    )
+    lines = 2 * received_ref.shape[0] * 8
+    spread = spread.reshape(lines, LANES).astype(BF16)
+    strips = jnp.concatenate(
+        [x.reshape(lines, LANES).astype(BF16) for x in parts] + [spread], axis=1
+    )
     sums = lax.dot_general(
-        received_ref[:, columns:],
-        received_ref[...],
-        (((0,), (0,)), ((), ())),
-        preferred_element_type=F32,
-    )[SPREAD : SPREAD + TROWS]
+        spread, strips, (((0,), (0,)), ((), ())), preferred_element_type=F32
+    )[:TROWS]
     coverage = sums[:, columns + ONE : columns + ONE + 1]
     template = sums / (1.0 + coverage)
-    edges = template[:, columns:]
+    edges = pltpu.roll(template[:, columns:], TURN, 1)
+    left = LANES - REACH
     upper, lower = split(jnp.concatenate([edges, template[:, :columns], edges], axis=1))
-    left = EXTRA - REACH
     upper_taps = jnp.concatenate([upper[:, left + a : left + a + columns] for a in range(TAPS)])
     lower_taps = jnp.concatenate([lower[:, left + a : left + a + columns] for a in range(TAPS)])
     basis = jnp.dot(
@@ -214,56 +261,54 @@
 
 def pack(strips, strip_patch, strip_row, strip_weight, peers):
     lines, columns = strips.shape
-    notes = jnp.stack([x.astype(F32) for x in (strip_patch, strip_row, strip_weight)])
+    about = jnp.stack([x.astype(F32) for x in (strip_patch, strip_row, strip_weight)])
     return call(
         pack_kernel,
         [
-            ((peers * SLOTS, columns + EXTRA), BF16),
+            ((peers // 2, TILES, 8, LANES), BF16),
             ((1, lines), jnp.int32),
-            ((lines, EXTRA), BF16),
+            ((lines, LANES), BF16),
+            ((lines, LANES), BF16),
         ],
         strips,
-        notes,
-        grid=(1,),
-        out_specs=[
-            pl.BlockSpec((peers * SLOTS, columns), lambda i: (0, 0)),
-            pl.BlockSpec((1, lines), lambda i: (0, 0)),
-            pl.BlockSpec((lines, EXTRA), lambda i: (0, 0)),
-        ],
+        about,
         cost_estimate=pl.CostEstimate(flops=10**9, bytes_accessed=2 * 10**6, transcendentals=0),
     )
 
 
-def add_edges(payload, key, extra, before, after):
-    rows, wide = payload.shape
+def add_notes(payload, key, notes, second, before, after):
+    pairs = payload.shape[0]
     lines = key.shape[1]
-    block = pl.BlockSpec((rows, EXTRA), lambda i: (0, wide // EXTRA - 1))
-    whole = pl.BlockSpec((lines, EXTRA), lambda i: (0, 0))
+    whole = pl.BlockSpec((lines, LANES), lambda i: (0, 0))
     (payload,) = call(
-        edge_kernel,
+        notes_kernel,
         [(payload.shape, BF16)],
         key,
-        extra,
+        notes,
+        second,
         before,
         after,
         payload,
         grid=(1,),
-        in_specs=[pl.BlockSpec((1, lines), lambda i: (0, 0)), whole, whole, whole]
+        in_specs=[pl.BlockSpec((1, lines), lambda i: (0, 0)), whole, whole, whole, whole]
         + [pl.BlockSpec(memory_space=pl.ANY)],
-        out_specs=[block],
-        input_output_aliases={4: 0},
+        out_specs=[pl.BlockSpec((pairs, 1, 8, LANES), lambda i: (0, NOTES, 0, 0))],
+        input_output_aliases={5: 0},
     )
     return payload
 
 
-def fit(received, science):
+def fit(odd, received, science):
     rows, columns = science.shape
     return call(
         fit_kernel,
         [((rows, columns), F32), ((1, UNKNOWNS), F32)],
+        odd,
         received,
         science,
         jnp.asarray(tap_table()),
+        in_specs=[pl.BlockSpec(memory_space=pltpu.SMEM)]
+        + [pl.BlockSpec(memory_space=pltpu.VMEM)] * 3,
         scratch_shapes=[
             pltpu.VMEM((ROWS, KP, columns), F32),
             pltpu.VMEM((2 * KP, ROWS * columns), BF16),
@@ -277,22 +322,20 @@
     count, lines, columns = strips.shape
     up = [(i, i + 1) for i in range(devices - 1)]
     down = [(j, i) for i, j in up]
-    last = strips[:, :, columns - EXTRA :].reshape(count * lines, EXTRA)
-    first = strips[:, :, :EXTRA].reshape(count * lines, EXTRA)
+    last = strips[:, :, columns - LANES :].reshape(count * lines, LANES)
+    first = strips[:, :, :LANES].reshape(count * lines, LANES)
     before = lax.ppermute(last, "det", up)
     after = lax.ppermute(first, "det", down)
-    payload, key, extra = pack(
+    payload, *notes = pack(
         strips.reshape(count * lines, columns), strip_patch, strip_row, strip_weight, peers
     )
-    payload = add_edges(payload, key, extra, before, after)
+    odd = (lax.axis_index("patch") & 1).reshape(1)
+    payload, odd = lax.optimization_barrier((payload, odd))
+    payload = add_notes(payload, *notes, before, after)
     received = lax.all_to_all(
-        payload.reshape(peers, SLOTS, columns + EXTRA),
-        "patch",
-        split_axis=0,
-        concat_axis=0,
-        tiled=True,
-    ).reshape(peers * SLOTS, columns + EXTRA)
-    difference, coefficients = fit(received, science[0])
+        payload.reshape(peers * TILES, 4, LANES), "patch", split_axis=0, concat_axis=0, tiled=True
+    ).reshape(payload.shape)
+    difference, coefficients = fit(odd, received, science[0])
     return (difference[None], coefficients[None])
 
 

time: 71.3 us -> 69 us (0.968)
  blocking collectives: 55 us -> 52.5 us
    all_to_all x1, blocking collectives: 55 us -> 52.5 us  [body(): lax.all_to_all(payload.reshape(peers * TILES, 4, LANES), 'patch', split_a...]
  transfers between devices with their start and end apart: 2 -> 2, of which waited for: 1 -> 1; matrix products, arithmetic and copies ran while one was open for 3% -> 4% of each run, Pallas kernels for 1% -> 1%
where the time goes in v5:
time: 69 us; the launch traced here: 68.7 us
  blocking collectives  52.5 us (76%)
  Pallas kernels  6.25 us (9%)
  starting transfers between devices  5.23 us (8%)
  local copies, waits for them, and re-layouts  2.12 us (3%)
  other arithmetic  1.35 us (2%)
  between operations  0.7 us (1%)
    all_to_all x1, blocking collectives, body(): lax.all_to_all(payload.reshape(peers * TILES, 4, LANES), 'patch', split_a...  52.5 us
    pallas_call x3, Pallas kernels, call(): pl.pallas_call(kernel, out_shape=[jax.ShapeDtypeStruct(shape, dtype) for...  6.25 us
    ppermute x1, starting transfers between devices, body(): before = lax.ppermute(last, 'det', up)  3.94 us
  transfers between devices with their start and end apart: 2, of which 1 were waited for; matrix products, arithmetic and copies ran while one was open for 4% of the time, Pallas kernels for 1%

profile of v5, /device:TPU:1, one launch (start us, length us, event | category | flops | bytes accessed | tf_op | source)
XLA Modules:
  0.0 68.7 jit_solution(5906916981527635796)
XLA Ops:
  0.6 1.0 %fusion = (bf16[96,4,128]{2,1,0:T(4,128)(2,1)S(1)}, bf16[96,4,128]{2,1,0:T(4,128)(2,1)S(1)}) fusion(bf16[96,4,512]{2,1,0:T(4,128)(2,1)} %param.6), kind=kLoop, calls=%fused_computation.4 | loop fusion | bytes 393216 | tf_op jit(solution)/shard_map/slice | solution.py:326
  1.6 3.9 %collective-permute-start = (bf16[384,128]{1,0:T(8,128)(2,1)S(1)}, bf16[384,128]{1,0:T(8,128)(2,1)S(1)}, u32[]{:S(2)}, u32[]{:S(2)}) collective-permute-start(bf16[384,128]{1,0:T(8,128)(2,1)S(1)} %bitcast.19), channel_id=1, source_target_pairs={{0,1},{1,2},{2,3},{4,5},{5,6},{6,7},{8,9},{9,10},{10,11},{12,13},{... | collective-permute-start | bytes 294920 | tf_op jit(solution)/shard_map/ppermute | solution.py:327
  5.6 1.3 %collective-permute-start.1 = (bf16[384,128]{1,0:T(8,128)(2,1)S(1)}, bf16[384,128]{1,0:T(8,128)(2,1)S(1)}, u32[]{:S(2)}, u32[]{:S(2)}) collective-permute-start(bf16[384,128]{1,0:T(8,128)(2,1)S(1)} %bitcast.18), channel_id=1, source_target_pairs={{1,0},{2,1},{3,2},{5,4},{6,5},{7,6},{9,8},{10,9},{11,10},{13,12},{... | collective-permute-start | bytes 294920 | tf_op jit(solution)/shard_map/ppermute | solution.py:328
  6.9 0.7 bitcast_convert_fusion
  7.6 0.7 convert_bitcast_fusion
  8.2 1.1 %reshape.22.strips_ref = bf16[384,512]{1,0:T(8,128)(2,1)S(1)} reshape(bf16[96,4,512]{2,1,0:T(4,128)(2,1)} %param.6) | data formatting | bytes 786432 | tf_op jit(solution)/shard_map/reshape | solution.py:330
  9.3 1.0 %pack_kernel.1 = (bf16[64,9,8,128]{3,2,1,0:T(8,128)(2,1)S(1)}, s32[1,384]{1,0:T(1,128)S(1)}, bf16[384,128]{1,0:T(8,128)(2,1)S(1)}, bf16[384,128]{1,0:T(8,128)(2,1)S(1)}) custom-call(bf16[384,512]{1,0:T(8,128)(2,1)S(1)} %reshape.22.strips_ref, f32[3,96]{1,0:T(4,128)S(1)} %pad_maximum_fusion.about_ref), custom_call_target="tpu_custom_call" | custom-call | flops 1000000000 | bytes 2000000 | tf_op jit(solution)/shard_map/pack_kernel/pallas_call | solution.py:253
  10.3 0.0 collective-permute-done.before_ref
  10.3 0.6 collective-permute-done.1.after_ref
  11.0 0.4 notes_kernel.1
  11.4 0.0 copy-start
  11.4 0.0 copy-start.1
  11.4 52.5 %all_to_all.5 = bf16[1152,4,128]{2,1,0:T(4,128)(2,1)S(1)} all-to-all(bf16[1152,4,128]{2,1,0:T(4,128)(2,1)S(1)} %bitcast.15), channel_id=1, replica_groups=mesh['patch'=128,'det'=4] {'patch'}, dimensions={0} | all-to-all | bytes 2359296 | tf_op jit(solution)/shard_map/all_to_all | solution.py:335
  63.9 0.0 copy-done
  63.9 0.0 copy-done.1
  63.9 4.9 %fit_kernel.1 = (f32[8,512]{1,0:T(8,128)}, f32[1,46]{1,0:T(1,128)}) custom-call(s32[1]{0:T(128)} %bitcast.3.odd_ref, bf16[64,9,8,128]{3,2,1,0:T(8,128)(2,1)S(1)} %bitcast.16, f32[8,512]{1,0:T(8,128)S(1)} %bitcast.17, bf16[384,2016]{1,0:T(8,128)(2,1)S(1)} %copy-done), custom_call_target="tpu_custom_call" | custom-call | tf_op jit(solution)/shard_map/fit_kernel/pallas_call | solution.py:253
  (1 shorter events, 0.0 us)
Async XLA Ops:
  1.6 8.7 %collective-permute-start = (bf16[384,128]{1,0:T(8,128)(2,1)S(1)}, bf16[384,128]{1,0:T(8,128)(2,1)S(1)}, u32[]{:S(2)}, u32[]{:S(2)}) collective-permute-start(bf16[384,128]{1,0:T(8,128)(2,1)S(1)} %bitcast.19), channel_id=1, source_target_pairs={{0,1},{1,2},{2,3},{4,5},{5,6},{6,7},{8,9},{9,10},{10,11},{12,13},{... | collective-permute-start | bytes 294920 | tf_op jit(solution)/shard_map/ppermute | solution.py:327
  5.6 5.4 %collective-permute-start.1 = (bf16[384,128]{1,0:T(8,128)(2,1)S(1)}, bf16[384,128]{1,0:T(8,128)(2,1)S(1)}, u32[]{:S(2)}, u32[]{:S(2)}) collective-permute-start(bf16[384,128]{1,0:T(8,128)(2,1)S(1)} %bitcast.18), channel_id=1, source_target_pairs={{1,0},{2,1},{3,2},{5,4},{6,5},{7,6},{9,8},{10,9},{11,10},{13,12},{... | collective-permute-start | bytes 294920 | tf_op jit(solution)/shard_map/ppermute | solution.py:328
  11.4 52.5 %copy-start = (bf16[384,2016]{1,0:T(8,128)(2,1)S(1)}, bf16[384,2016]{1,0:T(8,128)(2,1)}, u32[]{:S(2)}) copy-start(bf16[384,2016]{1,0:T(8,128)(2,1)} %constant.10.clone.table_ref) | copy-start | bytes 4644868
  11.4 52.5 %copy-start.1 = (f32[1,8,512]{2,1,0:T(8,128)S(1)}, f32[1,8,512]{2,1,0:T(8,128)}, u32[]{:S(2)}) copy-start(f32[1,8,512]{2,1,0:T(8,128)} %param.10) | copy-start | bytes 49156

commit v6 on v5

--- a/solution.py
+++ b/solution.py
@@ -17,9 +17,9 @@
 TILES = 9
 NOTES = 4
 HALF = 64
-EDGE = 32
-ONE = 52
-TURN = 86
+BEFORE = 32
+AFTER = 48
+ONE = 60
 KP = 48
 UNKNOWNS = BASIS + 1
 VMEM_LIMIT = 12 * 2**20
@@ -64,7 +64,7 @@
     return (iota(shape, 0) + base == key).astype(F32).astype(BF16)
 
 
-def pack_kernel(strips_ref, about_ref, out_ref, key_ref, notes_ref, second_ref):
+def pack_kernel(strips_ref, about_ref, out_ref, key_ref, notes_ref, slot_ref):
     count = about_ref.shape[1]
     patch_row, row_row, weight_row = (about_ref[i : i + 1, :] for i in range(3))
     lines, columns = strips_ref.shape
@@ -75,13 +75,21 @@
     earlier = (patch == patch_col) & (first < second)
     slot = jnp.sum(jnp.where(earlier, 1.0, 0.0), axis=0, keepdims=True)
     spread = (iota((count, lines), 1) // reps == iota((count, lines), 0)).astype(F32).astype(BF16)
-    wide = jnp.dot(
-        jnp.where(iota((8, count), 0) == 0, 2.0 * patch_row + slot, patch_row).astype(BF16),
-        spread,
-        preferred_element_type=F32,
-    ).astype(jnp.int32) * reps + iota((8, lines), 1) % reps
-    key = wide[:1]
-    key_ref[...] = wide[1:2]
+    facts = jnp.concatenate(
+        [2.0 * patch_row + slot, patch_row, row_row, slot, weight_row, jnp.zeros((3, count), F32)]
+    )
+    wide = jnp.dot(facts.astype(BF16), spread, preferred_element_type=F32)
+    line = iota((1, lines), 1) % reps
+    key = wide[:1].astype(jnp.int32) * reps + line
+    key_ref[...] = wide[1:2].astype(jnp.int32) * reps + line
+    slot_ref[...] = wide[3:4]
+    start = wide[3:4].astype(jnp.int32) * HALF
+    place = iota((LANES, lines), 0)
+    notes_ref[...] = jnp.where(
+        place == start + wide[2:3].astype(jnp.int32) + line,
+        wide[4:5],
+        jnp.where(place == start + ONE, 1.0, 0.0),
+    ).astype(BF16)
     strips = strips_ref[...]
     step = 256
     pairs = step // 16
@@ -93,35 +101,32 @@
                 out_ref[i * pairs : (i + 1) * pairs, c + odd * (NOTES + 1)] = picked[
                     :, odd, :, c * LANES : (c + 1) * LANES
                 ].astype(BF16)
-    here = iota((lines, count), 0) // reps == iota((lines, count), 1)
-
-    def line_of(values):
-        return jnp.sum(jnp.where(here, values, 0.0), axis=1, keepdims=True)
-
-    lane = iota((lines, LANES), 1)
-    start = line_of(slot).astype(jnp.int32) * HALF
-    at = start + line_of(row_row).astype(jnp.int32) + iota((lines, LANES), 0) % reps
-    notes_ref[...] = jnp.where(
-        lane == at, line_of(weight_row), jnp.where(lane == start + ONE, 1.0, 0.0)
-    ).astype(BF16)
-    second_ref[...] = jnp.broadcast_to(line_of(slot), (lines, LANES)).astype(BF16)
-
-
-def notes_kernel(key_ref, notes_ref, second_ref, before_ref, after_ref, unused_ref, out_ref):
-    lane = iota(notes_ref.shape, 1)
-    edges = jnp.where(
-        lane < REACH,
-        after_ref[...].astype(F32),
-        jnp.where(lane >= LANES - REACH, before_ref[...].astype(F32), 0.0),
-    )
-    edges = pltpu.roll(edges, LANES - TURN, 1)
-    edges = jnp.where(second_ref[...].astype(F32) > 0.5, pltpu.roll(edges, HALF, 1), edges)
+
+
+def notes_kernel(key_ref, notes_ref, slot_ref, before_ref, after_ref, unused_ref, out_ref):
+    lines = key_ref.shape[1]
+
+    def padded(edge, rows):
+        return [edge.astype(F32), jnp.zeros((rows - REACH, lines), F32)]
+
+    edges = jnp.concatenate(
+        [jnp.zeros((BEFORE, lines), F32)]
+        + padded(before_ref[...], AFTER - BEFORE)
+        + padded(after_ref[...], HALF - AFTER)
+    )
+    slot = slot_ref[...]
+    edges = jnp.concatenate([jnp.where(slot < 0.5, edges, 0.0), jnp.where(slot > 0.5, edges, 0.0)])
     notes = (notes_ref[...].astype(F32) + edges).astype(BF16)
     key = key_ref[...]
     step = 256
     pairs = step // 8
     for i in range(out_ref.shape[0] // pairs):
-        picked = jnp.dot(pick_rows(key, i * step, step), notes, preferred_element_type=F32)
+        picked = lax.dot_general(
+            pick_rows(key, i * step, step),
+            notes,
+            (((1,), (1,)), ((), ())),
+            preferred_element_type=F32,
+        )
         out_ref[i * pairs : (i + 1) * pairs, 0] = picked.reshape(pairs, 8, LANES).astype(BF16)
 
 
@@ -201,9 +206,10 @@
     )[:TROWS]
     coverage = sums[:, columns + ONE : columns + ONE + 1]
     template = sums / (1.0 + coverage)
-    edges = pltpu.roll(template[:, columns:], TURN, 1)
+    edges = template[:, columns:]
+    edges = (pltpu.roll(edges, LANES - REACH - BEFORE, 1), pltpu.roll(edges, LANES - AFTER, 1))
     left = LANES - REACH
-    upper, lower = split(jnp.concatenate([edges, template[:, :columns], edges], axis=1))
+    upper, lower = split(jnp.concatenate([edges[0], template[:, :columns], edges[1]], axis=1))
     upper_taps = jnp.concatenate([upper[:, left + a : left + a + columns] for a in range(TAPS)])
     lower_taps = jnp.concatenate([lower[:, left + a : left + a + columns] for a in range(TAPS)])
     basis = jnp.dot(
@@ -267,8 +273,8 @@
         [
             ((peers // 2, TILES, 8, LANES), BF16),
             ((1, lines), jnp.int32),
-            ((lines, LANES), BF16),
-            ((lines, LANES), BF16),
+            ((LANES, lines), BF16),
+            ((1, lines), F32),
         ],
         strips,
         about,
@@ -276,24 +282,17 @@
     )
 
 
-def add_notes(payload, key, notes, second, before, after):
-    pairs = payload.shape[0]
-    lines = key.shape[1]
-    whole = pl.BlockSpec((lines, LANES), lambda i: (0, 0))
+def add_notes(payload, *parts):
     (payload,) = call(
         notes_kernel,
         [(payload.shape, BF16)],
-        key,
-        notes,
-        second,
-        before,
-        after,
+        *parts,
         payload,
         grid=(1,),
-        in_specs=[pl.BlockSpec((1, lines), lambda i: (0, 0)), whole, whole, whole, whole]
+        in_specs=[pl.BlockSpec(x.shape, lambda i: (0, 0)) for x in parts]
         + [pl.BlockSpec(memory_space=pl.ANY)],
-        out_specs=[pl.BlockSpec((pairs, 1, 8, LANES), lambda i: (0, NOTES, 0, 0))],
-        input_output_aliases={5: 0},
+        out_specs=[pl.BlockSpec((payload.shape[0], 1, 8, LANES), lambda i: (0, NOTES, 0, 0))],
+        input_output_aliases={len(parts): 0},
     )
     return payload
 
@@ -322,8 +321,8 @@
     count, lines, columns = strips.shape
     up = [(i, i + 1) for i in range(devices - 1)]
     down = [(j, i) for i, j in up]
-    last = strips[:, :, columns - LANES :].reshape(count * lines, LANES)
-    first = strips[:, :, :LANES].reshape(count * lines, LANES)
+    last = strips[:, :, columns - REACH :].reshape(count * lines, REACH).T
+    first = strips[:, :, :REACH].reshape(count * lines, REACH).T
     before = lax.ppermute(last, "det", up)
     after = lax.ppermute(first, "det", down)
     payload, *notes = pack(

time: 69 us -> 68.3 us (0.990)
  other arithmetic: 1.35 us -> 0.02 us
    another operation x3, other arithmetic: 1.35 us -> 0.02 us  [pack(): jnp.stack([x.astype(F32) for x in (strip_patch, strip_row, strip_weight)])]
  transfers between devices with their start and end apart: 2 -> 2, of which waited for: 1 -> 1; matrix products, arithmetic and copies ran while one was open for 4% -> 2% of each run, Pallas kernels for 1% -> 1%
where the time goes in v6:
time: 68.3 us; the launch traced here: 68 us
  blocking collectives  52.5 us (77%)
  Pallas kernels  6.15 us (9%)
  starting transfers between devices  5.24 us (8%)
  local copies, waits for them, and re-layouts  2.37 us (3%)
  waiting for transfers between devices  0.99 us (1%)
  between operations  0.78 us (1%)
    all_to_all x1, blocking collectives, body(): lax.all_to_all(payload.reshape(peers * TILES, 4, LANES), 'patch', split_a...  52.5 us
    pallas_call x3, Pallas kernels, call(): pl.pallas_call(kernel, out_shape=[jax.ShapeDtypeStruct(shape, dtype) for...  6.15 us
    ppermute x1, starting transfers between devices, body(): before = lax.ppermute(last, 'det', up)  3.94 us
  transfers between devices with their start and end apart: 2, of which 1 were waited for; matrix products, arithmetic and copies ran while one was open for 2% of the time, Pallas kernels for 1%

profile of v6, /device:TPU:1, one launch (start us, length us, event | category | flops | bytes accessed | tf_op | source)
XLA Modules:
  0.0 68.0 jit_solution(16747335609840353388)
XLA Ops:
  0.6 0.0 copy-start.4
  0.6 0.0 copy-start.2
  0.7 0.0 copy-start.3
  0.7 1.1 %fusion = (bf16[96,4,10]{2,1,0:T(4,128)(2,1)S(1)}, bf16[96,4,10]{2,1,0:T(4,128)(2,1)S(1)}) fusion(bf16[96,4,512]{2,1,0:T(4,128)(2,1)} %param.6), kind=kLoop, calls=%fused_computation.4 | loop fusion | bytes 30720 | tf_op jit(solution)/shard_map/slice | solution.py:325
  1.7 0.1 copy.11
  1.8 3.9 %collective-permute-start = (bf16[10,384]{1,0:T(8,128)(2,1)S(1)}, bf16[10,384]{1,0:T(8,128)(2,1)S(1)}, u32[]{:S(2)}, u32[]{:S(2)}) collective-permute-start(bf16[10,384]{1,0:T(8,128)(2,1)S(1)} %bitcast.22), channel_id=1, source_target_pairs={{0,1},{1,2},{2,3},{4,5},{5,6},{6,7},{8,9},{9,10},{10,11},{12,13},{... | collective-permute-start | bytes 23048 | tf_op jit(solution)/shard_map/ppermute | solution.py:326
  5.8 0.1 copy.12
  5.9 1.3 %collective-permute-start.1 = (bf16[10,384]{1,0:T(8,128)(2,1)S(1)}, bf16[10,384]{1,0:T(8,128)(2,1)S(1)}, u32[]{:S(2)}, u32[]{:S(2)}) collective-permute-start(bf16[10,384]{1,0:T(8,128)(2,1)S(1)} %bitcast.23), channel_id=1, source_target_pairs={{1,0},{2,1},{3,2},{5,4},{6,5},{7,6},{9,8},{10,9},{11,10},{13,12},{... | collective-permute-start | bytes 23048 | tf_op jit(solution)/shard_map/ppermute | solution.py:327
  7.2 1.1 %reshape.22.strips_ref = bf16[384,512]{1,0:T(8,128)(2,1)S(1)} reshape(bf16[96,4,512]{2,1,0:T(4,128)(2,1)} %param.6) | data formatting | bytes 786432 | tf_op jit(solution)/shard_map/reshape | solution.py:329
  8.3 0.0 copy-done.4
  8.3 0.0 copy-done.2
  8.3 0.0 copy-done.3
  8.4 1.0 %pack_kernel.1 = (bf16[64,9,8,128]{3,2,1,0:T(8,128)(2,1)S(1)}, s32[1,384]{1,0:T(1,128)S(1)}, bf16[128,384]{1,0:T(8,128)(2,1)S(1)}, f32[1,384]{1,0:T(1,128)S(1)}) custom-call(bf16[384,512]{1,0:T(8,128)(2,1)S(1)} %reshape.22.strips_ref, f32[3,96]{1,0:T(4,128)S(1)} %pad_maximum_fusion.about_ref), custom_call_target="tpu_custom_call" | custom-call | flops 1000000000 | bytes 2000000 | tf_op jit(solution)/shard_map/pack_kernel/pallas_call | solution.py:259
  9.3 0.0 collective-permute-done.before_ref
  9.3 1.0 %collective-permute-done.1.after_ref = bf16[10,384]{1,0:T(8,128)(2,1)S(1)} collective-permute-done((bf16[10,384]{1,0:T(8,128)(2,1)S(1)}, bf16[10,384]{1,0:T(8,128)(2,1)S(1)}, u32[]{:S(2)}, u32[]{:S(2)}) %collective-permute-start.1) | collective-permute-done | bytes 7712 | tf_op jit(solution)/shard_map/ppermute | solution.py:327
  10.3 0.3 notes_kernel.1
  10.7 0.0 copy-start
  10.7 0.0 copy-start.1
  10.7 52.5 %all_to_all.5 = bf16[1152,4,128]{2,1,0:T(4,128)(2,1)S(1)} all-to-all(bf16[1152,4,128]{2,1,0:T(4,128)(2,1)S(1)} %bitcast.18), channel_id=1, replica_groups=mesh['patch'=128,'det'=4] {'patch'}, dimensions={0} | all-to-all | bytes 2359296 | tf_op jit(solution)/shard_map/all_to_all | solution.py:334
  63.1 0.0 copy-done
  63.1 0.0 copy-done.1
  63.1 4.9 %fit_kernel.1 = (f32[8,512]{1,0:T(8,128)}, f32[1,46]{1,0:T(1,128)}) custom-call(s32[1]{0:T(128)} %bitcast.3.odd_ref, bf16[64,9,8,128]{3,2,1,0:T(8,128)(2,1)S(1)} %bitcast.17, f32[8,512]{1,0:T(8,128)S(1)} %bitcast.19, bf16[384,2016]{1,0:T(8,128)(2,1)S(1)} %copy-done), custom_call_target="tpu_custom_call" | custom-call | tf_op jit(solution)/shard_map/fit_kernel/pallas_call | solution.py:259
  (3 shorter events, 0.0 us)
Async XLA Ops:
  0.6 7.7 %copy-start.4 = (bf16[96]{0:T(256)(128)(2,1)S(1)}, bf16[96]{0:T(256)(128)(2,1)}, u32[]{:S(2)}) copy-start(bf16[96]{0:T(256)(128)(2,1)} %param.9) | copy-start | bytes 580
  0.6 7.7 %copy-start.2 = (s32[96]{0:T(128)S(1)}, s32[96]{0:T(128)}, u32[]{:S(2)}) copy-start(s32[96]{0:T(128)} %param.8) | copy-start | bytes 1156
  0.7 7.7 %copy-start.3 = (s32[96]{0:T(128)S(1)}, s32[96]{0:T(128)}, u32[]{:S(2)}) copy-start(s32[96]{0:T(128)} %param.7) | copy-start | bytes 1156
  1.8 7.5 %collective-permute-start = (bf16[10,384]{1,0:T(8,128)(2,1)S(1)}, bf16[10,384]{1,0:T(8,128)(2,1)S(1)}, u32[]{:S(2)}, u32[]{:S(2)}) collective-permute-start(bf16[10,384]{1,0:T(8,128)(2,1)S(1)} %bitcast.22), channel_id=1, source_target_pairs={{0,1},{1,2},{2,3},{4,5},{5,6},{6,7},{8,9},{9,10},{10,11},{12,13},{... | collective-permute-start | bytes 23048 | tf_op jit(solution)/shard_map/ppermute | solution.py:326
  5.9 4.4 %collective-permute-start.1 = (bf16[10,384]{1,0:T(8,128)(2,1)S(1)}, bf16[10,384]{1,0:T(8,128)(2,1)S(1)}, u32[]{:S(2)}, u32[]{:S(2)}) collective-permute-start(bf16[10,384]{1,0:T(8,128)(2,1)S(1)} %bitcast.23), channel_id=1, source_target_pairs={{1,0},{2,1},{3,2},{5,4},{6,5},{7,6},{9,8},{10,9},{11,10},{13,12},{... | collective-permute-start | bytes 23048 | tf_op jit(solution)/shard_map/ppermute | solution.py:327
  10.7 52.5 %copy-start = (bf16[384,2016]{1,0:T(8,128)(2,1)S(1)}, bf16[384,2016]{1,0:T(8,128)(2,1)}, u32[]{:S(2)}) copy-start(bf16[384,2016]{1,0:T(8,128)(2,1)} %constant.10.clone.table_ref) | copy-start | bytes 4644868
  10.7 52.5 %copy-start.1 = (f32[1,8,512]{2,1,0:T(8,128)S(1)}, f32[1,8,512]{2,1,0:T(8,128)}, u32[]{:S(2)}) copy-start(f32[1,8,512]{2,1,0:T(8,128)} %param.10) | copy-start | bytes 49156

commit v7 on v6

--- a/solution.py
+++ b/solution.py
@@ -47,7 +47,7 @@
     table = table.reshape(ROWS * KP, TAPS * TROWS).astype(np.float32)
     high = table.astype(BF16)
     low = (table - high.astype(np.float32)).astype(BF16)
-    return np.concatenate([high, high, low], axis=1)
+    return np.concatenate([high, low])
 
 
 def iota(shape, dim):
@@ -212,10 +212,10 @@
     upper, lower = split(jnp.concatenate([edges[0], template[:, :columns], edges[1]], axis=1))
     upper_taps = jnp.concatenate([upper[:, left + a : left + a + columns] for a in range(TAPS)])
     lower_taps = jnp.concatenate([lower[:, left + a : left + a + columns] for a in range(TAPS)])
-    basis = jnp.dot(
-        table_ref[...],
-        jnp.concatenate([upper_taps, lower_taps, upper_taps]),
-        preferred_element_type=F32,
+    tall = jnp.dot(table_ref[...], upper_taps, preferred_element_type=F32)
+    basis = tall[: ROWS * KP] + (
+        tall[ROWS * KP :]
+        + jnp.dot(table_ref[: ROWS * KP], lower_taps, preferred_element_type=F32)
     )
     science = science_ref[...]
     place = iota((8, columns), 0)

time: 68.3 us -> 68 us (level)
  no operation moved by 1% of the time
where the time goes in v7:
time: 68 us; the launch traced here: 67.8 us
  blocking collectives  52.5 us (77%)
  Pallas kernels  5.91 us (9%)
  starting transfers between devices  5.24 us (8%)
  local copies, waits for them, and re-layouts  2.37 us (3%)
  waiting for transfers between devices  0.99 us (1%)
  between operations  0.78 us (1%)
    all_to_all x1, blocking collectives, body(): lax.all_to_all(payload.reshape(peers * TILES, 4, LANES), 'patch', split_a...  52.5 us
    pallas_call x3, Pallas kernels, call(): pl.pallas_call(kernel, out_shape=[jax.ShapeDtypeStruct(shape, dtype) for...  5.91 us
    ppermute x1, starting transfers between devices, body(): before = lax.ppermute(last, 'det', up)  3.94 us
  transfers between devices with their start and end apart: 2, of which 1 were waited for; matrix products, arithmetic and copies ran while one was open for 2% of the time, Pallas kernels for 1%

profile of v7, /device:TPU:1, one launch (start us, length us, event | category | flops | bytes accessed | tf_op | source)
XLA Modules:
  0.0 67.8 jit_solution(2254833735639681559)
XLA Ops:
  0.6 0.0 copy-start.4
  0.6 0.0 copy-start.2
  0.7 0.0 copy-start.3
  0.7 1.1 %fusion = (bf16[96,4,10]{2,1,0:T(4,128)(2,1)S(1)}, bf16[96,4,10]{2,1,0:T(4,128)(2,1)S(1)}) fusion(bf16[96,4,512]{2,1,0:T(4,128)(2,1)} %param.6), kind=kLoop, calls=%fused_computation.4 | loop fusion | bytes 30720 | tf_op jit(solution)/shard_map/slice | solution.py:325
  1.7 0.1 copy.11
  1.8 3.9 %collective-permute-start = (bf16[10,384]{1,0:T(8,128)(2,1)S(1)}, bf16[10,384]{1,0:T(8,128)(2,1)S(1)}, u32[]{:S(2)}, u32[]{:S(2)}) collective-permute-start(bf16[10,384]{1,0:T(8,128)(2,1)S(1)} %bitcast.22), channel_id=1, source_target_pairs={{0,1},{1,2},{2,3},{4,5},{5,6},{6,7},{8,9},{9,10},{10,11},{12,13},{... | collective-permute-start | bytes 23048 | tf_op jit(solution)/shard_map/ppermute | solution.py:326
  5.8 0.1 copy.12
  5.9 1.3 %collective-permute-start.1 = (bf16[10,384]{1,0:T(8,128)(2,1)S(1)}, bf16[10,384]{1,0:T(8,128)(2,1)S(1)}, u32[]{:S(2)}, u32[]{:S(2)}) collective-permute-start(bf16[10,384]{1,0:T(8,128)(2,1)S(1)} %bitcast.23), channel_id=1, source_target_pairs={{1,0},{2,1},{3,2},{5,4},{6,5},{7,6},{9,8},{10,9},{11,10},{13,12},{... | collective-permute-start | bytes 23048 | tf_op jit(solution)/shard_map/ppermute | solution.py:327
  7.2 1.1 %reshape.22.strips_ref = bf16[384,512]{1,0:T(8,128)(2,1)S(1)} reshape(bf16[96,4,512]{2,1,0:T(4,128)(2,1)} %param.6) | data formatting | bytes 786432 | tf_op jit(solution)/shard_map/reshape | solution.py:329
  8.3 0.0 copy-done.4
  8.3 0.0 copy-done.2
  8.3 0.0 copy-done.3
  8.4 1.0 %pack_kernel.1 = (bf16[64,9,8,128]{3,2,1,0:T(8,128)(2,1)S(1)}, s32[1,384]{1,0:T(1,128)S(1)}, bf16[128,384]{1,0:T(8,128)(2,1)S(1)}, f32[1,384]{1,0:T(1,128)S(1)}) custom-call(bf16[384,512]{1,0:T(8,128)(2,1)S(1)} %reshape.22.strips_ref, f32[3,96]{1,0:T(4,128)S(1)} %pad_maximum_fusion.about_ref), custom_call_target="tpu_custom_call" | custom-call | flops 1000000000 | bytes 2000000 | tf_op jit(solution)/shard_map/pack_kernel/pallas_call | solution.py:259
  9.3 0.0 collective-permute-done.before_ref
  9.3 1.0 %collective-permute-done.1.after_ref = bf16[10,384]{1,0:T(8,128)(2,1)S(1)} collective-permute-done((bf16[10,384]{1,0:T(8,128)(2,1)S(1)}, bf16[10,384]{1,0:T(8,128)(2,1)S(1)}, u32[]{:S(2)}, u32[]{:S(2)}) %collective-permute-start.1) | collective-permute-done | bytes 7712 | tf_op jit(solution)/shard_map/ppermute | solution.py:327
  10.3 0.3 notes_kernel.1
  10.7 0.0 copy-start
  10.7 0.0 copy-start.1
  10.7 52.5 %all_to_all.5 = bf16[1152,4,128]{2,1,0:T(4,128)(2,1)S(1)} all-to-all(bf16[1152,4,128]{2,1,0:T(4,128)(2,1)S(1)} %bitcast.17), channel_id=1, replica_groups=mesh['patch'=128,'det'=4] {'patch'}, dimensions={0} | all-to-all | bytes 2359296 | tf_op jit(solution)/shard_map/all_to_all | solution.py:334
  63.1 0.0 copy-done
  63.1 0.0 copy-done.1
  63.1 4.6 %fit_kernel.1 = (f32[8,512]{1,0:T(8,128)}, f32[1,46]{1,0:T(1,128)}) custom-call(s32[1]{0:T(128)} %bitcast.3.odd_ref, bf16[64,9,8,128]{3,2,1,0:T(8,128)(2,1)S(1)} %bitcast.18, f32[8,512]{1,0:T(8,128)S(1)} %bitcast.19, bf16[768,672]{1,0:T(8,128)(2,1)S(1)} %copy-done), custom_call_target="tpu_custom_call" | custom-call | tf_op jit(solution)/shard_map/fit_kernel/pallas_call | solution.py:259
  (3 shorter events, 0.0 us)
Async XLA Ops:
  0.6 7.7 %copy-start.4 = (bf16[96]{0:T(256)(128)(2,1)S(1)}, bf16[96]{0:T(256)(128)(2,1)}, u32[]{:S(2)}) copy-start(bf16[96]{0:T(256)(128)(2,1)} %param.9) | copy-start | bytes 580
  0.6 7.7 %copy-start.2 = (s32[96]{0:T(128)S(1)}, s32[96]{0:T(128)}, u32[]{:S(2)}) copy-start(s32[96]{0:T(128)} %param.8) | copy-start | bytes 1156
  0.7 7.7 %copy-start.3 = (s32[96]{0:T(128)S(1)}, s32[96]{0:T(128)}, u32[]{:S(2)}) copy-start(s32[96]{0:T(128)} %param.7) | copy-start | bytes 1156
  1.8 7.5 %collective-permute-start = (bf16[10,384]{1,0:T(8,128)(2,1)S(1)}, bf16[10,384]{1,0:T(8,128)(2,1)S(1)}, u32[]{:S(2)}, u32[]{:S(2)}) collective-permute-start(bf16[10,384]{1,0:T(8,128)(2,1)S(1)} %bitcast.22), channel_id=1, source_target_pairs={{0,1},{1,2},{2,3},{4,5},{5,6},{6,7},{8,9},{9,10},{10,11},{12,13},{... | collective-permute-start | bytes 23048 | tf_op jit(solution)/shard_map/ppermute | solution.py:326
  5.9 4.4 %collective-permute-start.1 = (bf16[10,384]{1,0:T(8,128)(2,1)S(1)}, bf16[10,384]{1,0:T(8,128)(2,1)S(1)}, u32[]{:S(2)}, u32[]{:S(2)}) collective-permute-start(bf16[10,384]{1,0:T(8,128)(2,1)S(1)} %bitcast.23), channel_id=1, source_target_pairs={{1,0},{2,1},{3,2},{5,4},{6,5},{7,6},{9,8},{10,9},{11,10},{13,12},{... | collective-permute-start | bytes 23048 | tf_op jit(solution)/shard_map/ppermute | solution.py:327
  10.7 52.5 %copy-start = (bf16[768,672]{1,0:T(8,128)(2,1)S(1)}, bf16[768,672]{1,0:T(8,128)(2,1)}, u32[]{:S(2)}) copy-start(bf16[768,672]{1,0:T(8,128)(2,1)} %constant.10.clone.table_ref) | copy-start | bytes 3096580
  10.7 52.5 %copy-start.1 = (f32[1,8,512]{2,1,0:T(8,128)S(1)}, f32[1,8,512]{2,1,0:T(8,128)}, u32[]{:S(2)}) copy-start(f32[1,8,512]{2,1,0:T(8,128)} %param.10) | copy-start | bytes 49156

commit v8 on v7

--- a/solution.py
+++ b/solution.py
@@ -117,17 +117,11 @@
     slot = slot_ref[...]
     edges = jnp.concatenate([jnp.where(slot < 0.5, edges, 0.0), jnp.where(slot > 0.5, edges, 0.0)])
     notes = (notes_ref[...].astype(F32) + edges).astype(BF16)
-    key = key_ref[...]
-    step = 256
-    pairs = step // 8
-    for i in range(out_ref.shape[0] // pairs):
-        picked = lax.dot_general(
-            pick_rows(key, i * step, step),
-            notes,
-            (((1,), (1,)), ((), ())),
-            preferred_element_type=F32,
-        )
-        out_ref[i * pairs : (i + 1) * pairs, 0] = picked.reshape(pairs, 8, LANES).astype(BF16)
+    rows = out_ref.shape[0] * 8
+    picked = lax.dot_general(
+        pick_rows(key_ref[...], 0, rows), notes, (((1,), (1,)), ((), ())), preferred_element_type=F32
+    )
+    out_ref[:, 0] = picked.reshape(out_ref.shape[0], 8, LANES).astype(BF16)
 
 
 def invert_pair(a, b, d):

time: 68 us -> 68 us (level)
  no operation moved by 1% of the time
where the time goes in v8:
time: 68 us; the launch traced here: 67.7 us
  blocking collectives  52.5 us (77%)
  Pallas kernels  5.88 us (9%)
  starting transfers between devices  5.24 us (8%)
  local copies, waits for them, and re-layouts  2.37 us (3%)
  waiting for transfers between devices  0.99 us (1%)
  between operations  0.78 us (1%)
    all_to_all x1, blocking collectives, body(): lax.all_to_all(payload.reshape(peers * TILES, 4, LANES), 'patch', split_a...  52.5 us
    pallas_call x3, Pallas kernels, call(): pl.pallas_call(kernel, out_shape=[jax.ShapeDtypeStruct(shape, dtype) for...  5.88 us
    ppermute x1, starting transfers between devices, body(): before = lax.ppermute(last, 'det', up)  3.94 us
  transfers between devices with their start and end apart: 2, of which 1 were waited for; matrix products, arithmetic and copies ran while one was open for 2% of the time, Pallas kernels for 1%

profile of v8, /device:TPU:1, one launch (start us, length us, event | category | flops | bytes accessed | tf_op | source)
XLA Modules:
  0.0 67.7 jit_solution(16390086162088130955)
XLA Ops:
  0.6 0.0 copy-start.4
  0.6 0.0 copy-start.2
  0.7 0.0 copy-start.3
  0.7 1.1 %fusion = (bf16[96,4,10]{2,1,0:T(4,128)(2,1)S(1)}, bf16[96,4,10]{2,1,0:T(4,128)(2,1)S(1)}) fusion(bf16[96,4,512]{2,1,0:T(4,128)(2,1)} %param.6), kind=kLoop, calls=%fused_computation.4 | loop fusion | bytes 30720 | tf_op jit(solution)/shard_map/slice | solution.py:319
  1.7 0.1 copy.11
  1.8 3.9 %collective-permute-start = (bf16[10,384]{1,0:T(8,128)(2,1)S(1)}, bf16[10,384]{1,0:T(8,128)(2,1)S(1)}, u32[]{:S(2)}, u32[]{:S(2)}) collective-permute-start(bf16[10,384]{1,0:T(8,128)(2,1)S(1)} %bitcast.22), channel_id=1, source_target_pairs={{0,1},{1,2},{2,3},{4,5},{5,6},{6,7},{8,9},{9,10},{10,11},{12,13},{... | collective-permute-start | bytes 23048 | tf_op jit(solution)/shard_map/ppermute | solution.py:320
  5.8 0.1 copy.12
  5.9 1.3 %collective-permute-start.1 = (bf16[10,384]{1,0:T(8,128)(2,1)S(1)}, bf16[10,384]{1,0:T(8,128)(2,1)S(1)}, u32[]{:S(2)}, u32[]{:S(2)}) collective-permute-start(bf16[10,384]{1,0:T(8,128)(2,1)S(1)} %bitcast.23), channel_id=1, source_target_pairs={{1,0},{2,1},{3,2},{5,4},{6,5},{7,6},{9,8},{10,9},{11,10},{13,12},{... | collective-permute-start | bytes 23048 | tf_op jit(solution)/shard_map/ppermute | solution.py:321
  7.2 1.1 %reshape.22.strips_ref = bf16[384,512]{1,0:T(8,128)(2,1)S(1)} reshape(bf16[96,4,512]{2,1,0:T(4,128)(2,1)} %param.6) | data formatting | bytes 786432 | tf_op jit(solution)/shard_map/reshape | solution.py:323
  8.3 0.0 copy-done.4
  8.3 0.0 copy-done.2
  8.3 0.0 copy-done.3
  8.4 1.0 %pack_kernel.1 = (bf16[64,9,8,128]{3,2,1,0:T(8,128)(2,1)S(1)}, s32[1,384]{1,0:T(1,128)S(1)}, bf16[128,384]{1,0:T(8,128)(2,1)S(1)}, f32[1,384]{1,0:T(1,128)S(1)}) custom-call(bf16[384,512]{1,0:T(8,128)(2,1)S(1)} %reshape.22.strips_ref, f32[3,96]{1,0:T(4,128)S(1)} %pad_maximum_fusion.about_ref), custom_call_target="tpu_custom_call" | custom-call | flops 1000000000 | bytes 2000000 | tf_op jit(solution)/shard_map/pack_kernel/pallas_call | solution.py:253
  9.3 0.0 collective-permute-done.before_ref
  9.3 1.0 %collective-permute-done.1.after_ref = bf16[10,384]{1,0:T(8,128)(2,1)S(1)} collective-permute-done((bf16[10,384]{1,0:T(8,128)(2,1)S(1)}, bf16[10,384]{1,0:T(8,128)(2,1)S(1)}, u32[]{:S(2)}, u32[]{:S(2)}) %collective-permute-start.1) | collective-permute-done | bytes 7712 | tf_op jit(solution)/shard_map/ppermute | solution.py:321
  10.3 0.3 notes_kernel.1
  10.6 0.0 copy-start
  10.6 0.0 copy-start.1
  10.7 52.5 %all_to_all.5 = bf16[1152,4,128]{2,1,0:T(4,128)(2,1)S(1)} all-to-all(bf16[1152,4,128]{2,1,0:T(4,128)(2,1)S(1)} %bitcast.17), channel_id=1, replica_groups=mesh['patch'=128,'det'=4] {'patch'}, dimensions={0} | all-to-all | bytes 2359296 | tf_op jit(solution)/shard_map/all_to_all | solution.py:328
  63.1 0.0 copy-done
  63.1 0.0 copy-done.1
  63.1 4.6 %fit_kernel.1 = (f32[8,512]{1,0:T(8,128)}, f32[1,46]{1,0:T(1,128)}) custom-call(s32[1]{0:T(128)} %bitcast.3.odd_ref, bf16[64,9,8,128]{3,2,1,0:T(8,128)(2,1)S(1)} %bitcast.18, f32[8,512]{1,0:T(8,128)S(1)} %bitcast.19, bf16[768,672]{1,0:T(8,128)(2,1)S(1)} %copy-done), custom_call_target="tpu_custom_call" | custom-call | tf_op jit(solution)/shard_map/fit_kernel/pallas_call | solution.py:253
  (3 shorter events, 0.0 us)
Async XLA Ops:
  0.6 7.7 %copy-start.4 = (bf16[96]{0:T(256)(128)(2,1)S(1)}, bf16[96]{0:T(256)(128)(2,1)}, u32[]{:S(2)}) copy-start(bf16[96]{0:T(256)(128)(2,1)} %param.9) | copy-start | bytes 580
  0.6 7.7 %copy-start.2 = (s32[96]{0:T(128)S(1)}, s32[96]{0:T(128)}, u32[]{:S(2)}) copy-start(s32[96]{0:T(128)} %param.8) | copy-start | bytes 1156
  0.7 7.7 %copy-start.3 = (s32[96]{0:T(128)S(1)}, s32[96]{0:T(128)}, u32[]{:S(2)}) copy-start(s32[96]{0:T(128)} %param.7) | copy-start | bytes 1156
  1.8 7.5 %collective-permute-start = (bf16[10,384]{1,0:T(8,128)(2,1)S(1)}, bf16[10,384]{1,0:T(8,128)(2,1)S(1)}, u32[]{:S(2)}, u32[]{:S(2)}) collective-permute-start(bf16[10,384]{1,0:T(8,128)(2,1)S(1)} %bitcast.22), channel_id=1, source_target_pairs={{0,1},{1,2},{2,3},{4,5},{5,6},{6,7},{8,9},{9,10},{10,11},{12,13},{... | collective-permute-start | bytes 23048 | tf_op jit(solution)/shard_map/ppermute | solution.py:320
  5.9 4.4 %collective-permute-start.1 = (bf16[10,384]{1,0:T(8,128)(2,1)S(1)}, bf16[10,384]{1,0:T(8,128)(2,1)S(1)}, u32[]{:S(2)}, u32[]{:S(2)}) collective-permute-start(bf16[10,384]{1,0:T(8,128)(2,1)S(1)} %bitcast.23), channel_id=1, source_target_pairs={{1,0},{2,1},{3,2},{5,4},{6,5},{7,6},{9,8},{10,9},{11,10},{13,12},{... | collective-permute-start | bytes 23048 | tf_op jit(solution)/shard_map/ppermute | solution.py:321
  10.6 52.5 %copy-start = (bf16[768,672]{1,0:T(8,128)(2,1)S(1)}, bf16[768,672]{1,0:T(8,128)(2,1)}, u32[]{:S(2)}) copy-start(bf16[768,672]{1,0:T(8,128)(2,1)} %constant.10.clone.table_ref) | copy-start | bytes 3096580
  10.6 52.5 %copy-start.1 = (f32[1,8,512]{2,1,0:T(8,128)S(1)}, f32[1,8,512]{2,1,0:T(8,128)}, u32[]{:S(2)}) copy-start(f32[1,8,512]{2,1,0:T(8,128)} %param.10) | copy-start | bytes 49156
